TPU v7x, 128 devices: a whole 4x4x4 slice. The times are simulated.
128 devices in a mesh: prow: 8 (over z, core), pcol: 16 (over x, y).
Axes of the slice: x: 4, y: 4, z: 4, core: 2. Of those that a mesh axis runs over, the one named last changes fastest.
Arguments:
- panel_pos: float32 [3, 256], replicated
- trail_pos: float32 [3, 8192], P(None, ('prow', 'pcol')), as said below
- slot_block: int32 [32], replicated, may hold values from 0 to 31, each once
Outputs:
- panel_diag: float32 [768, 768], replicated
- panel_below: float32 [24576, 768], P(('prow', 'pcol'))
- trailing: float32 [24576, 24576], P('prow', 'pcol')
Inputs may be any that keep to these rules, and one draw needn't show every extreme that they name: `slot_block`: every trailing panel is named by exactly one slot. Any two particles of panel_pos and trail_pos together are 0.5 or more apart.
All inputs are finite; a program needn't handle non-finite values.
Results may differ from a plain program's by a relative error of at most 0.0003.
Values sent between devices are 32-bit elements; how exact they have to be, the bound alone decides.
A program may use at most 192 MiB of HBM per device.

v0:
```python
import jax
import jax.numpy as jnp
from jax import lax
from jax.sharding import PartitionSpec as P

PB = 256


radius = 0.25


def from_root(value, axis, source):
    kept = jnp.where(lax.axis_index(axis) == source, value, 0).astype(value.dtype)
    return lax.psum(kept, axis)


def pair_terms(difference, same_particle):
    squared = jnp.sum(difference * difference, axis=0)
    safe_square = jnp.where(same_particle, 1.0, squared)
    inverse_r = lax.rsqrt(safe_square)
    radius_ratio = radius * radius * inverse_r * inverse_r
    isotropic = jnp.where(
        same_particle, 1.0, 0.75 * radius * inverse_r * (1.0 + radius_ratio * 2.0 / 3.0)
    )
    directed = jnp.where(
        same_particle,
        0.0,
        0.75 * radius * inverse_r * inverse_r * inverse_r * (1.0 - 2.0 * radius_ratio),
    )
    return (isotropic, directed)


def block_tiles(row_pos, row_ids, col_pos, col_ids):
    difference = row_pos[:, :, :, None, None] - col_pos[:, None, None, :, :]
    same_particle = row_ids[:, :, None, None] == col_ids[None, None, :, :]
    isotropic, directed = pair_terms(difference, same_particle)
    identity = jnp.eye(3, dtype=difference.dtype)
    tensor = (
        identity[:, :, None, None, None, None] * isotropic[None, None]
        + directed[None, None] * difference[:, None] * difference[None, :]
    )
    tensor = jnp.transpose(tensor, (2, 0, 3, 4, 1, 5))
    return tensor.reshape(row_pos.shape[1] * 3 * PB, col_pos.shape[1] * 3 * PB)


def row_tiles(row_pos, component, panel):
    difference = row_pos[:, :, None] - panel[:, None, :]
    same_particle = jnp.zeros(difference.shape[1:], dtype=jnp.bool_)
    isotropic, directed = pair_terms(difference, same_particle)
    select = (component[None, :] == lax.iota(jnp.int32, 3)[:, None]).astype(difference.dtype)
    projected = jnp.sum(select[:, :, None] * difference, axis=0)
    tensor = select[:, :, None] * isotropic[None] + directed[None] * projected[None] * difference
    return jnp.transpose(tensor, (1, 0, 2)).reshape(row_pos.shape[1], 3 * PB)


def row_layout(global_rows):
    width = 3 * PB
    block_index = global_rows // width
    within = global_rows % width
    component = within // PB
    particle = block_index * PB + within % PB
    return (component, particle)


def outer_rows(left_rows, right_rows):
    return lax.dot_general(
        left_rows,
        right_rows,
        (((1,), (1,)), ((), ())),
        precision=lax.Precision.HIGHEST,
        preferred_element_type=jnp.float32,
    )


def shards(panel_pos, trail_pos, slot_block):
    width = 3 * PB
    row_devices = lax.axis_size("prow")
    col_devices = lax.axis_size("pcol")
    row_index = lax.axis_index("prow")
    col_index = lax.axis_index("pcol")
    panels = slot_block.shape[0]
    all_positions = lax.all_gather(trail_pos, ("prow", "pcol"), axis=1, tiled=True)
    sorted_pos = all_positions.reshape(3, panels, PB)[:, slot_block].reshape(3, panels * PB)
    panel_ids = lax.iota(jnp.int32, PB).reshape(1, PB)
    diag_block = block_tiles(
        panel_pos.reshape(3, 1, PB), panel_ids, panel_pos.reshape(3, 1, PB), panel_ids
    )
    factor = jnp.linalg.cholesky(diag_block)
    inverse = jax.scipy.linalg.solve_triangular(
        factor, jnp.eye(width, dtype=factor.dtype), lower=True
    )
    span_rows = panels * width // row_devices
    span_cols = panels * width // col_devices
    share = span_cols // row_devices
    row_first = row_index * span_rows
    col_first = col_index * span_cols
    blocks = sorted_pos.reshape(3, panels, PB)
    slot_ids = lax.iota(jnp.int32, panels * PB).reshape(panels, PB)
    row_blocks = span_rows // width
    col_blocks = span_cols // width
    row_pos = lax.dynamic_slice_in_dim(blocks, row_index * row_blocks, row_blocks, 1)
    row_ids = lax.dynamic_slice_in_dim(slot_ids, row_index * row_blocks, row_blocks, 0)
    col_pos = lax.dynamic_slice_in_dim(blocks, col_index * col_blocks, col_blocks, 1)
    col_ids = lax.dynamic_slice_in_dim(slot_ids, col_index * col_blocks, col_blocks, 0)
    pair_tiles = block_tiles(row_pos, row_ids, col_pos, col_ids)
    component, particle = row_layout(row_first + col_index * share + lax.iota(jnp.int32, share))
    below_block = row_tiles(jnp.take(sorted_pos, particle, axis=1), component, panel_pos)
    own_rows = outer_rows(below_block, inverse)
    left_rows = lax.all_gather(own_rows, "pcol", axis=0, tiled=True)
    owner_row = col_first // span_rows
    offset = col_first % span_rows
    matching = lax.dynamic_slice_in_dim(left_rows, offset, span_cols, 0)
    right_rows = from_root(matching, "prow", owner_row)
    trailing = pair_tiles - outer_rows(left_rows, right_rows)
    return (factor, own_rows, trailing)


def solution(mesh):
    return jax.shard_map(
        shards,
        mesh=mesh,
        in_specs=(P(), P(None, ("prow", "pcol")), P()),
        out_specs=(P(), P(("prow", "pcol"), None), P("prow", "pcol")),
        check_vma=False,
    )
```

profile of v0, /device:TPU:0, one launch (start us, length us, event | category | flops | bytes accessed | tf_op | source)
XLA Modules:
  0.0 557.6 jit_solution(18307448556489717698)
XLA Ops:
  11.0 62.9 %all-gather = f32[128,64,3]{1,2,0:T(4,128)S(1)} all-gather(f32[1,64,3]{1,2,0:T(4,128)S(1)} %bitcast.122), channel_id=1, replica_groups=mesh['prow'=8,'pcol'=16] {'prow','pcol'}, dimensions={0}, use_global_device_ids=true | all-gather | bytes 99072 | tf_op jit(solution)/shard_map/all_gather | solution.py:82
  74.7 2.7 copy.58
  77.4 2.9 gather_fusion.1
  89.4 11.7 %cholesky.165 = f32[128,128]{1,0:T(8,128)S(1)} custom-call(f32[128,128]{1,0:T(8,128)S(1)} %cholesky.424), custom_call_target="Cholesky" | custom-call | tf_op jit(solution)/shard_map/jit(cholesky)/cholesky | solution.py:88
  101.3 9.8 %custom-call.47 = f32[1,128,128]{1,2,0:T(8,128)S(1)} custom-call(f32[1,128,128]{2,1,0:T(8,128)S(1)} %get-tuple-element.58), custom_call_target="InvertDiagBlocksLowerTriangular" | custom-call | tf_op jit(solution)/shard_map/jit(cholesky)/cholesky | solution.py:88
  114.5 13.2 %cholesky.188 = f32[128,128]{1,0:T(8,128)} custom-call(f32[128,128]{1,0:T(8,128)} %cholesky.428), custom_call_target="Cholesky" | custom-call | tf_op jit(solution)/shard_map/jit(cholesky)/cholesky | solution.py:88
  129.2 11.5 %custom-call.48 = f32[1,128,128]{1,2,0:T(8,128)} custom-call(f32[1,128,128]{2,1,0:T(8,128)} %get-tuple-element.55), custom_call_target="InvertDiagBlocksLowerTriangular" | custom-call | tf_op jit(solution)/shard_map/jit(cholesky)/cholesky | solution.py:88
  144.0 12.5 %cholesky.354 = f32[128,128]{1,0:T(8,128)S(1)} custom-call(f32[128,128]{1,0:T(8,128)} %cholesky.433), custom_call_target="Cholesky" | custom-call | tf_op jit(solution)/shard_map/jit(cholesky)/cholesky | solution.py:88
  157.2 10.6 %custom-call.49 = f32[1,128,128]{1,2,0:T(8,128)S(1)} custom-call(f32[1,128,128]{2,1,0:T(8,128)} %get-tuple-element.52), custom_call_target="InvertDiagBlocksLowerTriangular" | custom-call | tf_op jit(solution)/shard_map/jit(cholesky)/cholesky | solution.py:88
  169.8 12.1 %cholesky.373 = f32[128,128]{1,0:T(8,128)S(1)} custom-call(f32[128,128]{1,0:T(8,128)S(1)} %cholesky.438), custom_call_target="Cholesky" | custom-call | tf_op jit(solution)/shard_map/jit(cholesky)/cholesky | solution.py:88
  181.9 9.8 %custom-call.50 = f32[1,128,128]{1,2,0:T(8,128)S(1)} custom-call(f32[1,128,128]{2,1,0:T(8,128)S(1)} %get-tuple-element.49), custom_call_target="InvertDiagBlocksLowerTriangular" | custom-call | tf_op jit(solution)/shard_map/jit(cholesky)/cholesky | solution.py:88
  193.5 11.7 %cholesky.392 = f32[128,128]{1,0:T(8,128)S(1)} custom-call(f32[128,128]{1,0:T(8,128)S(1)} %cholesky.443), custom_call_target="Cholesky" | custom-call | tf_op jit(solution)/shard_map/jit(cholesky)/cholesky | solution.py:88
  205.3 9.8 %custom-call.51 = f32[1,128,128]{1,2,0:T(8,128)S(1)} custom-call(f32[1,128,128]{2,1,0:T(8,128)S(1)} %get-tuple-element.46), custom_call_target="InvertDiagBlocksLowerTriangular" | custom-call | tf_op jit(solution)/shard_map/jit(cholesky)/cholesky | solution.py:88
  216.6 11.9 %cholesky.410 = f32[128,128]{1,0:T(8,128)S(1)} custom-call(f32[128,128]{1,0:T(8,128)S(1)} %convolution_subtract_fusion.9), custom_call_target="Cholesky" | custom-call | tf_op jit(solution)/shard_map/jit(cholesky)/cholesky | solution.py:88
  238.2 21.6 %while.1 = (s32[]{:T(128)}, f32[768,768]{1,0:T(8,128)}, s32[6,2]{0,1:T(2,128)S(1)}, f32[6,128,128]{2,1,0:T(8,128)}, s32[]{:T(128)}) while((s32[]{:T(128)}, f32[768,768]{1,0:T(8,128)}, s32[6,2]{0,1:T(2,128)S(1)}, f32[6,128,128]{2,1,0:T(8,128)}, s32[]{:T(128)}) %tuple.51), condition=%wide.while_cond, body=%wide.while_body.sunk | while | flops 2 | bytes 132205 | solution.py:89
  238.9 3.0 bitcast_dynamic-update-slice_fusion.2
  242.5 2.9 bitcast_dynamic-update-slice_fusion.2
  246.2 2.9 bitcast_dynamic-update-slice_fusion.2
  249.8 2.9 bitcast_dynamic-update-slice_fusion.2
  253.4 2.9 bitcast_dynamic-update-slice_fusion.2
  257.0 2.9 bitcast_dynamic-update-slice_fusion.2
  259.9 60.4 %custom-call.52 = f32[6,128,128]{1,2,0:T(8,128)} custom-call(f32[6,128,128]{2,1,0:T(8,128)} %get-tuple-element.10), custom_call_target="InvertDiagBlocksLowerTriangular" | custom-call | tf_op jit(solution)/shard_map/jit(_solve_triangular)/triangular_solve | solution.py:89
  340.3 5.0 fusion.27
  349.8 2.9 copy.62
  352.8 4.0 broadcast_subtract_fusion
  356.8 62.4 %all-gather.3.cloned.1.call-done = f32[3072,768]{1,0:T(8,128)} async-done(((f32[192,768]{1,0:T(8,128)}), f32[3072,768]{1,0:T(8,128)}) %all-gather.3.cloned.1.call-update) | async-done | bytes 9437200 | tf_op jit(solution)/shard_map/all_gather | solution.py:109
  419.2 4.9 dynamic-slice_select_fusion
  424.1 5.5 subtract_multiply_fusion
  429.6 14.9 %multiply_add_fusion = f32[4,3,256,2,3,256]{5,4,3,2,1,0:T(4,128)} fusion(f32[4,256,2,3,256]{4,3,2,1,0:T(4,128)} %broadcast_subtract_fusion, f32[4,3,256,2,256]{4,3,2,1,0:T(2,128)} %subtract_multiply_fusion, f32[4,256,2,256]{3,2,1,0:T(2,128)} %copy.62, f32[3,3]{1,0:T(4,128)S(1)} %fusion.68), kind=kLoop, calls=%fused_computation.4 | loop fusion | flops 14155776 | bytes 33554468 | tf_op jit(solution)/shard_map/add | solution.py:39
  444.4 30.6 %add.269 = f32[3072,1536]{1,0:T(8,128)} reshape(f32[4,3,256,2,3,256]{5,4,3,2,1,0:T(4,128)} %multiply_add_fusion) | data formatting | bytes 37748736 | tf_op jit(solution)/shard_map/add | solution.py:39
  475.0 23.6 %all-reduce.3.cloned.1.call-done = f32[1536,768]{1,0:T(8,128)} async-done(((f32[1536,768]{1,0:T(8,128)}), f32[1536,768]{1,0:T(8,128)}) %all-reduce.3.cloned.1.call-update) | async-done | bytes 4718608 | tf_op jit(solution)/shard_map/psum | solution.py:14
  498.6 51.9 %convolution_subtract_fusion = f32[3072,1536]{1,0:T(8,128)} fusion(f32[3072,1536]{1,0:T(8,128)} %add.269, f32[3072,768]{1,0:T(8,128)} %all-gather.3.cloned.1.call-done, f32[1536,768]{1,0:T(8,128)} %all-reduce.3.cloned.1.call-done), kind=kOutput, calls=%fused_computation.5 | convolution fusion | flops 43491262464 | bytes 51904512 | tf_op jit(solution)/shard_map/dot_general | solution.py:66
  (122 shorter events, 62.1 us)
Async XLA Ops:
  7.2 3.8 copy-start.6
  7.2 66.9 %copy-start.7 = (s32[32]{0:T(128)S(1)}, s32[32]{0:T(128)}, u32[]{:S(2)}) copy-start(s32[32]{0:T(128)} %param.5) | copy-start | bytes 388
  7.2 412.0 %all-gather.3.cloned.1.call-start = ((), (), s32[]{:S(2)}) async-start(), calls=%async_computation | async-start | bytes 10027008 | tf_op jit(solution)/shard_map/all_gather | solution.py:109
  74.7 7.0 %copy-start.5 = (f32[3,256]{1,0:T(4,128)S(1)}, f32[3,256]{1,0:T(4,128)}, u32[]{:S(2)}) copy-start(f32[3,256]{1,0:T(4,128)} %param.3) | copy-start | bytes 9220
  87.9 1.4 copy-start.1
  238.2 86.9 %copy-start = (f32[768,768]{1,0:T(8,128)S(1)}, f32[768,768]{1,0:T(8,128)}, u32[]{:S(2)}) copy-start(f32[768,768]{1,0:T(8,128)} %fusion.23) | copy-start | bytes 7077892
  320.2 3.6 copy-start.4
  332.9 3.6 copy-start.3
  336.9 0.9 copy-start.2
  345.3 153.2 %all-reduce.3.cloned.1.call-start = ((), (), s32[]{:S(2)}) async-start(), calls=%async_computation.1 | async-start | bytes 9437184 | tf_op jit(solution)/shard_map/psum | solution.py:14
Sparse Core Ops, SparseCore 0:
  345.4 73.6 all-gather.2
  424.2 74.2 all-reduce.2
where the time goes:
time: 564 us; the launch traced here: 558 us
  other arithmetic  233 us (41%)
  waiting for transfers between devices  86 us (15%)
  matrix products  85.9 us (15%)
  local copies, waits for them, and re-layouts  70.9 us (13%)
  blocking collectives  62.9 us (11%)
  between operations  18.7 us (3%)
    another operation x22, other arithmetic, shards(): factor = jnp.linalg.cholesky(diag_block)  130 us
    all_gather x1, blocking collectives, shards(): lax.all_gather(trail_pos, ('prow', 'pcol'), axis=1, tiled=True)  62.9 us
    another operation x3, other arithmetic, shards(): jax.scipy.linalg.solve_triangular(factor, jnp.eye(width, dtype=factor.dty...  62.9 us
    all_gather x1, waiting for transfers between devices, shards(): left_rows = lax.all_gather(own_rows, 'pcol', axis=0, tiled=True)  62.4 us
    dot_general x2, matrix products, outer_rows(): lax.dot_general(left_rows, right_rows, (((1,), (1,)), ((), ())), precisio...  57 us
    add x1, local copies, waits for them, and re-layouts, block_tiles(): identity[:, :, None, None, None, None] * isotropic[None, None]  30.6 us
    psum x1, waiting for transfers between devices, from_root(): return lax.psum(kept, axis)  23.6 us
    another operation x18, local copies, waits for them, and re-layouts  21.6 us
  transfers between devices with their start and end apart: 2, of which 2 were waited for; matrix products, arithmetic and copies ran while one was open for 11% of the time, Pallas kernels for 0%

commit v1 on v0

v1 whole, which is shorter than its diff:
```python
import functools
import jax
import jax.numpy as jnp
from jax import lax
from jax.experimental import pallas as pl
from jax.experimental.pallas import tpu as pltpu
from jax.sharding import PartitionSpec as P

RADIUS = 0.25
F32, BF16 = jnp.float32, jnp.bfloat16
NT = (((1,), (1,)), ((), ()))
NN = (((1,), (0,)), ((), ()))
TN = (((0,), (0,)), ((), ()))


def split(x):
    hi = x.astype(BF16)
    return hi, (x - hi.astype(F32)).astype(BF16)


def dot3(a, b, dims):
    ah, al = split(a)
    bh, bl = split(b)
    d = functools.partial(lax.dot_general, dimension_numbers=dims, preferred_element_type=F32)
    return d(ah, bh) + (d(al, bh) + d(ah, bl))


def pair_terms(rows, cols):
    diff = [r - c for r, c in zip(rows, cols)]
    squared = diff[0] * diff[0] + diff[1] * diff[1] + diff[2] * diff[2]
    same = squared < 0.01
    inv = lax.rsqrt(jnp.where(same, 1.0, squared))
    inv2 = inv * inv
    t = (0.75 * RADIUS) * inv
    t2 = t * inv2
    iso = jnp.where(same, 1.0, t + (RADIUS * RADIUS * 2.0 / 3.0) * t2)
    directed = t2 * (1.0 - (2.0 * RADIUS * RADIUS) * inv2)
    return diff, iso, directed


def tensor_entries(rows, cols):
    diff, iso, directed = pair_terms(rows, cols)
    g = [directed * d for d in diff]
    e = {}
    for i in range(3):
        for j in range(i, 3):
            v = g[i] * diff[j]
            if i == j:
                v = v + iso
            e[i, j] = e[j, i] = v
    return e


def bsub(row):
    return jnp.broadcast_to(row, (8, row.shape[-1]))


def factor_block(d_ref):
    sub = lax.broadcasted_iota(jnp.int32, (8, 128), 0)
    n = 16
    ta = [d_ref[8 * s : 8 * s + 8, :128] for s in range(n)]
    ti = [d_ref[8 * s : 8 * s + 8, 128:] for s in range(n)]
    for t in range(n):
        cs = {s: [jnp.broadcast_to(ta[s][:, 8 * t + k : 8 * t + k + 1], (8, 128)) for k in range(8)] for s in range(t, n)}
        for j in range(8):
            rs = lax.rsqrt(bsub(cs[t][j][j : j + 1, :]))
            mt = cs[t][j] * rs
            mm = jnp.where(sub > j, mt, 0.0)
            sp = {k: bsub(mt[k : k + 1, :]) for k in range(j + 1, 8)}
            ua = bsub(ta[t][j : j + 1, :]) * rs
            ui = bsub(ti[t][j : j + 1, :]) * rs
            ta[t] = jnp.where(sub == j, ua, ta[t] - mm * ua)
            ti[t] = jnp.where(sub == j, ui, ti[t] - mm * ui)
            for k in range(j + 1, 8):
                cs[t][k] = cs[t][k] - mm * sp[k]
            for s in range(t + 1, n):
                m = cs[s][j] * rs
                ta[s] = ta[s] - m * ua
                ti[s] = ti[s] - m * ui
                for k in range(j + 1, 8):
                    cs[s][k] = cs[s][k] - m * sp[k]
        d_ref[8 * t : 8 * t + 8, :128] = ta[t]
        d_ref[8 * t : 8 * t + 8, 128:] = ti[t]


def cat_store(ref, rows, chunk, hi, lo, order):
    base = 768 * chunk
    for i, w in enumerate(order):
        ref[rows, base + 256 * i : base + 256 * i + 256] = hi if w == "h" else lo


def chol(panel_ref, panel_t, m_ref, d_ref, l_ref, xcat):
    m_ref[:, 768:] = jnp.zeros((768, 768), F32)
    for r in range(0, 256, 32):
        rows = [panel_t[r : r + 32, c : c + 1] for c in range(3)]
        cols = [panel_ref[c : c + 1, :] for c in range(3)]
        e = tensor_entries(rows, cols)
        for i in range(3):
            for j in range(3):
                m_ref[256 * i + r : 256 * i + r + 32, 256 * j : 256 * j + 256] = e[i, j]
    eye = (lax.broadcasted_iota(jnp.int32, (128, 128), 0) == lax.broadcasted_iota(jnp.int32, (128, 128), 1)).astype(F32)
    upper = lax.broadcasted_iota(jnp.int32, (128, 128), 0) <= lax.broadcasted_iota(jnp.int32, (128, 128), 1)
    l_ref[...] = jnp.zeros((768, 768), F32)
    xcat[...] = jnp.zeros(xcat.shape, BF16)

    def panel(p, _):
        base = pl.multiple_of(128 * p, 128)
        nxt = pl.multiple_of(128 * p + 128, 128)
        d_ref[:, :128] = m_ref[pl.ds(base, 128), pl.ds(base, 128)]
        d_ref[:, 128:] = eye
        factor_block(d_ref)
        x = d_ref[:, 128:]
        row = dot3(x, m_ref[pl.ds(base, 128), pl.ds(nxt, 640)], NN)
        m_ref[pl.ds(base, 128), pl.ds(base, 128)] = jnp.where(upper, d_ref[:, :128], 0.0)
        m_ref[pl.ds(base, 128), pl.ds(nxt, 640)] = row
        m_ref[pl.ds(base, 128), pl.ds(768 + base, 128)] = x

        def update(r, _):
            at = pl.multiple_of(128 * r, 128)
            lt = m_ref[pl.ds(base, 128), pl.ds(at, 128)]
            m_ref[pl.ds(at, 128), pl.ds(nxt, 768)] -= dot3(lt, m_ref[pl.ds(base, 128), pl.ds(nxt, 768)], TN)
            return 0

        lax.fori_loop(p + 1, 6, update, 0)
        return 0

    lax.fori_loop(0, 6, panel, 0)
    for p in range(6):
        for q in range(p, 6):
            l_ref[128 * q : 128 * q + 128, 128 * p : 128 * p + 128] = m_ref[128 * p : 128 * p + 128, 128 * q : 128 * q + 128].T
    for k in range(3):
        hi, lo = split(m_ref[256 * k :, 768 + 256 * k : 1024 + 256 * k])
        cat_store(xcat, slice(256 * k, 768), k, hi, lo, "hhl")


def panel_rows(rows, panel_ref, bcat, xcat, emit):
    for r in range(0, 128, 32):
        e = tensor_entries(rows(r, 32), [panel_ref[c : c + 1, :] for c in range(3)])
        for i in range(3):
            for j in range(3):
                hi, lo = split(e[i, j])
                cat_store(bcat, slice(128 * i + r, 128 * i + r + 32), j, hi, lo, "hlh")
    for n in range(3):
        k = 768 * (n + 1)
        v = lax.dot_general(bcat[:, :k], xcat[256 * n : 256 * n + 256, :k], NT, preferred_element_type=F32)
        emit(n, v)


def kernel(slot_ref, panel_ref, g_ref, l_ref, own_ref, out_ref, m_ref, d_ref, xcat, ccat, rcat, bcat, rowt, colt, colp, pt, ids):
    step = pl.program_id(0)
    lane = lax.broadcasted_iota(jnp.int32, (8, 128), 1)
    prow, pcol = ids()

    def lane_tile(k, half):
        d = 4 * k + 2 * half
        a = jnp.concatenate([g_ref[(d % 16), d // 16], jnp.zeros((5, 64), F32)], axis=0)
        d = d + 1
        b = jnp.concatenate([g_ref[(d % 16), d // 16], jnp.zeros((5, 64), F32)], axis=0)
        return jnp.concatenate([a, b], axis=1)

    def transposed(tile):
        return jnp.concatenate([tile, jnp.zeros((120, 128), F32)], axis=0).T

    @pl.when(step == 0)
    def _():
        for half in range(2):
            tile = panel_ref[:, 128 * half : 128 * half + 128]
            pt[128 * half : 128 * half + 128, :] = transposed(tile)

        def rows_of(i, _):
            k = slot_ref[prow * 4 + i // 2]
            rowt[pl.ds(pl.multiple_of(i * 128, 128), 128), :] = transposed(lane_tile(k, i % 2))
            return 0

        lax.fori_loop(0, 8, rows_of, 0)
        for i in range(4):
            k = slot_ref[pcol * 2 + i // 2]
            tile = lane_tile(k, i % 2)
            colp[:, 128 * i : 128 * i + 128] = tile
            colt[128 * i : 128 * i + 128, :] = transposed(tile)
        chol(panel_ref, pt, m_ref, d_ref, l_ref, xcat)

        def col_rows(i, _):
            at = pl.multiple_of(i * 128, 128)
            dst = (i // 2) * 768 + (i % 2) * 128

            def emit(n, v):
                hi, lo = split(v)
                for j in range(3):
                    cat_store(ccat, pl.ds(pl.multiple_of(dst + 256 * j, 128), 128), n,
                              hi[128 * j : 128 * j + 128], lo[128 * j : 128 * j + 128], "hhl")

            panel_rows(lambda r, m: [colt[pl.ds(at + r, m), c : c + 1] for c in range(3)], panel_ref, bcat, xcat, emit)
            return 0

        lax.fori_loop(0, 4, col_rows, 0)

    c = step % 2
    tile = step // 2
    at = pl.multiple_of(tile * 128, 128)

    @pl.when(c == 0)
    def _():
        def emit(n, v):
            hi, lo = split(v)
            cat_store(rcat, slice(None), n, hi, lo, "hlh")
            for i in range(3):
                for h in range(2):
                    piece = i * 4 + (tile % 2) * 2 + h

                    @pl.when((tile // 2 == pcol // 4) & (piece // 3 == pcol % 4))
                    def _():
                        own_ref[pl.ds(pl.multiple_of((piece % 3) * 64, 64), 64), 256 * n : 256 * n + 256] = v[128 * i + 64 * h : 128 * i + 64 * h + 64]

        panel_rows(lambda r, m: [rowt[pl.ds(at + r, m), k : k + 1] for k in range(3)], panel_ref, bcat, xcat, emit)

    crow = pl.multiple_of(c * 768, 256)
    for j in range(3):
        v = lax.dot_general(rcat[...], ccat[pl.ds(crow + 256 * j, 256), :], NT, preferred_element_type=F32)
        out_ref[0, :, :, 256 * j : 256 * j + 256] = v.reshape(3, 128, 256)
    cc = pl.multiple_of(c * 256, 256)
    for r in range(0, 128, 32):
        rows = [rowt[pl.ds(at + r, 32), k : k + 1] for k in range(3)]
        cols = [colp[k : k + 1, pl.ds(cc, 256)] for k in range(3)]
        e = tensor_entries(rows, cols)
        for i in range(3):
            for j in range(3):
                out_ref[0, i, r : r + 32, 256 * j : 256 * j + 256] = e[i, j] - out_ref[0, i, r : r + 32, 256 * j : 256 * j + 256]


def main_call(slot_block, panel_pos, gathered, ids):
    panel8 = jnp.pad(panel_pos, ((0, 5), (0, 0)))
    whole = lambda s: (0, 0)
    l, own, out = pl.pallas_call(
        functools.partial(kernel, ids=ids),
        grid=(16,),
        in_specs=[
            pl.BlockSpec(memory_space=pltpu.SMEM),
            pl.BlockSpec((8, 256), whole),
            pl.BlockSpec((16, 8, 3, 64), lambda s: (0, 0, 0, 0)),
        ],
        out_specs=[
            pl.BlockSpec((768, 768), whole),
            pl.BlockSpec((192, 768), whole),
            pl.BlockSpec((1, 3, 128, 768), lambda s: (s // 4, 0, (s // 2) % 2, s % 2)),
        ],
        out_shape=[
            jax.ShapeDtypeStruct((768, 768), F32),
            jax.ShapeDtypeStruct((192, 768), F32),
            jax.ShapeDtypeStruct((4, 3, 256, 1536), F32),
        ],
        scratch_shapes=[
            pltpu.VMEM((768, 1536), F32),
            pltpu.VMEM((128, 256), F32),
            pltpu.VMEM((768, 2304), BF16),
            pltpu.VMEM((1536, 2304), BF16),
            pltpu.VMEM((384, 2304), BF16),
            pltpu.VMEM((384, 2304), BF16),
            pltpu.VMEM((1024, 128), F32),
            pltpu.VMEM((512, 128), F32),
            pltpu.VMEM((8, 512), F32),
            pltpu.VMEM((256, 128), F32),
        ],
        compiler_params=pltpu.CompilerParams(dimension_semantics=("arbitrary",), vmem_limit_bytes=62 << 20),
        name="panel_step",
    )(slot_block, panel8, gathered)
    return l, own, out.reshape(3072, 1536)


MESH = pl.DeviceIdType.MESH


def gather_kernel(n_rows, n_cols, own_ref, out_ref, send_sem, recv_sem, local_sem):
    r = lax.axis_index("prow")
    c = lax.axis_index("pcol")
    local = pltpu.make_async_copy(own_ref, out_ref.at[c, r], local_sem)
    local.start()
    barrier = pltpu.get_barrier_semaphore()
    for i in range(1, n_rows):
        pl.semaphore_signal(barrier, inc=1, device_id=(lax.rem(r + i, n_rows), c), device_id_type=MESH)
    for i in range(1, n_cols):
        pl.semaphore_signal(barrier, inc=1, device_id=(r, lax.rem(c + i, n_cols)), device_id_type=MESH)
    pl.semaphore_wait(barrier, n_rows + n_cols - 2)
    first = [
        pltpu.make_async_remote_copy(
            src_ref=own_ref,
            dst_ref=out_ref.at[c, r],
            send_sem=send_sem.at[i],
            recv_sem=recv_sem.at[i],
            device_id=(lax.rem(r + i, n_rows), c),
            device_id_type=MESH,
        )
        for i in range(1, n_rows)
    ]
    for copy in first:
        copy.start()
    local.wait()
    for copy in first:
        copy.wait()
    second = [
        pltpu.make_async_remote_copy(
            src_ref=out_ref.at[c],
            dst_ref=out_ref.at[c],
            send_sem=send_sem.at[n_rows + i],
            recv_sem=recv_sem.at[n_rows + i],
            device_id=(r, lax.rem(c + i, n_cols)),
            device_id_type=MESH,
        )
        for i in range(1, n_cols)
    ]
    for copy in second:
        copy.start()
    for copy in second:
        copy.wait()


def gather_positions(own):
    n_rows, n_cols = lax.axis_size("prow"), lax.axis_size("pcol")
    return pl.pallas_call(
        functools.partial(gather_kernel, n_rows, n_cols),
        out_shape=jax.ShapeDtypeStruct((n_cols, n_rows) + own.shape, own.dtype),
        in_specs=[pl.BlockSpec(memory_space=pltpu.VMEM)],
        out_specs=pl.BlockSpec(memory_space=pltpu.VMEM),
        scratch_shapes=[
            pltpu.SemaphoreType.DMA((n_rows + n_cols,)),
            pltpu.SemaphoreType.DMA((n_rows + n_cols,)),
            pltpu.SemaphoreType.DMA,
        ],
        compiler_params=pltpu.CompilerParams(collective_id=0, has_side_effects=True),
        name="gather_positions",
    )(own)


def shards(panel_pos, trail_pos, slot_block):
    gathered = gather_positions(trail_pos)
    return main_call(slot_block, panel_pos, gathered, lambda: (lax.axis_index("prow"), lax.axis_index("pcol")))


def solution(mesh):
    return jax.shard_map(
        shards,
        mesh=mesh,
        in_specs=(P(), P(None, ("prow", "pcol")), P()),
        out_specs=(P(), P(("prow", "pcol"), None), P("prow", "pcol")),
        check_vma=False,
    )
```

time: 564 us -> 109 us (0.19); the launches traced: 558 us -> 109 us
  other arithmetic: 233 us -> 0 us
  Pallas kernels: 0 us -> 107 us
  waiting for transfers between devices: 86 us -> 0 us
  matrix products: 85.9 us -> 0 us
  local copies, waits for them, and re-layouts: 70.9 us -> 1.29 us
  blocking collectives: 62.9 us -> 0 us
  between operations: 18.7 us -> 0.64 us
    another operation x25 -> x0, other arithmetic: 193 us -> none  [the longest x22 130 us: shards(): factor = jnp.linalg.cholesky(diag_block)]
    pallas_call x0 -> x2, Pallas kernels: none -> 107 us  [the longest x1 89.3 us: main_call(): pl.pallas_call(functools.partial(kernel, ids=ids), grid=(16,), in_specs=[...]
    all_gather x1 -> x0, blocking collectives: 62.9 us -> none  [shards(): lax.all_gather(trail_pos, ('prow', 'pcol'), axis=1, tiled=True)]
    all_gather x1 -> x0, waiting for transfers between devices: 62.4 us -> none  [shards(): left_rows = lax.all_gather(own_rows, 'pcol', axis=0, tiled=True)]
    dot_general x2 -> x0, matrix products: 57 us -> none  [outer_rows(): lax.dot_general(left_rows, right_rows, (((1,), (1,)), ((), ())), precisio...]
    add x1 -> x0, local copies, waits for them, and re-layouts: 30.6 us -> none  [block_tiles(): identity[:, :, None, None, None, None] * isotropic[None, None]]
    another operation x21 -> x0, matrix products: 28.9 us -> none  [the longest x11 18.3 us: shards(): jax.scipy.linalg.solve_triangular(factor, jnp.eye(width, dtype=factor.dty...]
    psum x1 -> x0, waiting for transfers between devices: 23.6 us -> none  [from_root(): return lax.psum(kept, axis)]
  transfers between devices with their start and end apart: 2 -> 0, of which waited for: 2 -> 0; matrix products, arithmetic and copies ran while one was open for 11% -> 0% of each run, Pallas kernels for 0% -> 0%
where the time goes in v1:
time: 109 us
  Pallas kernels  107 us (98%)
  local copies, waits for them, and re-layouts  1.29 us (1%)
    pallas_call x1, Pallas kernels, main_call(): pl.pallas_call(functools.partial(kernel, ids=ids), grid=(16,), in_specs=[...  89.3 us
    pallas_call x1, Pallas kernels, gather_positions(): pl.pallas_call(functools.partial(gather_kernel, n_rows, n_cols), out_shap...  17.9 us

profile of v1, /device:TPU:0, one launch (start us, length us, event | category | flops | bytes accessed | tf_op | source)
XLA Modules:
  0.0 109.2 jit_solution(11275198948361652185)
XLA Ops:
  0.6 1.3 %pad.4.panel_ref = f32[8,256]{1,0:T(8,128)} pad(f32[3,256]{1,0:T(4,128)} %param.3, f32[]{:T(128)} %constant.2.clone.1), padding=0_5x0_0 | pad | bytes 11268 | tf_op jit(solution)/shard_map/jit(_pad)/pad | solution.py:232
  1.9 17.9 %gather_positions.1.g_ref = f32[16,8,3,64]{3,2,1,0:T(4,128)} custom-call(f32[3,64]{1,0:T(4,128)} %own_ref.1), custom_call_target="tpu_custom_call" | custom-call | tf_op jit(solution)/shard_map/gather_positions/pallas_call | solution.py:319
  19.9 89.3 %panel_step.1 = (f32[768,768]{1,0:T(8,128)}, f32[192,768]{1,0:T(8,128)}, f32[4,3,256,1536]{3,2,1,0:T(8,128)}) custom-call(s32[32]{0:T(128)} %slot_ref.1, f32[8,256]{1,0:T(8,128)} %pad.4.panel_ref, f32[16,8,3,64]{3,2,1,0:T(4,128)} %gather_positions.1.g_ref), custom_call_target="tpu_custom_call" | custom-call | tf_op jit(solution)/shard_map/panel_step/pallas_call | solution.py:234

commit v2 on v0

v2 whole, which is shorter than its diff:
```python
import functools
import jax
import jax.numpy as jnp
from jax import lax
from jax.experimental import pallas as pl
from jax.experimental.pallas import tpu as pltpu
from jax.sharding import PartitionSpec as P

RADIUS = 0.25
F32, BF16, F8 = jnp.float32, jnp.bfloat16, jnp.float8_e4m3fn
NT = (((1,), (1,)), ((), ()))
NN = (((1,), (0,)), ((), ()))
TN = (((0,), (0,)), ((), ()))


def split(x):
    hi = x.astype(BF16)
    return hi, (x - hi.astype(F32)).astype(BF16)


def dot3(a, b, dims):
    ah, al = split(a)
    bh, bl = split(b)
    d = functools.partial(lax.dot_general, dimension_numbers=dims, preferred_element_type=F32)
    return d(ah, bh) + (d(al, bh) + d(ah, bl))


def pair_terms(rows, cols):
    diff = [r - c for r, c in zip(rows, cols)]
    squared = diff[0] * diff[0] + diff[1] * diff[1] + diff[2] * diff[2]
    same = squared < 0.01
    inv = lax.rsqrt(jnp.where(same, 1.0, squared))
    inv2 = inv * inv
    t = (0.75 * RADIUS) * inv
    t2 = t * inv2
    iso = jnp.where(same, 1.0, t + (RADIUS * RADIUS * 2.0 / 3.0) * t2)
    directed = t2 * (1.0 - (2.0 * RADIUS * RADIUS) * inv2)
    return diff, iso, directed


def tensor_entries(rows, cols):
    diff, iso, directed = pair_terms(rows, cols)
    g = [directed * d for d in diff]
    e = {}
    for i in range(3):
        for j in range(i, 3):
            v = g[i] * diff[j]
            if i == j:
                v = v + iso
            e[i, j] = e[j, i] = v
    return e


def bsub(row):
    return jnp.broadcast_to(row, (8, row.shape[-1]))


def rep(tile, rows):
    return jnp.concatenate([tile] * (rows // 8), axis=0)


def first_tile(tile, rest):
    return tile if rest.shape[0] == 8 else jnp.concatenate([tile, rest[8:]], axis=0)


def factor_block(d_ref):
    sub = lax.broadcasted_iota(jnp.int32, (8, 128), 0)
    a = d_ref[:, :128]
    inv = d_ref[:, 128:]
    for t in range(16):
        n = 128 - 8 * t
        cs = [jnp.broadcast_to(a[:, 8 * t + k : 8 * t + k + 1], (n, 128)) for k in range(8)]
        for j in range(8):
            rs = lax.rsqrt(bsub(cs[j][j : j + 1, :]))
            m = cs[j] * rep(rs, n)
            sp = [rep(bsub(m[k : k + 1, :]), n) for k in range(j + 1, 8)]
            m = first_tile(jnp.where(sub > j, m[:8], 0.0), m)
            ua = bsub(a[j : j + 1, :]) * rs
            ui = bsub(inv[j : j + 1, :]) * rs
            a = a - m * rep(ua, n)
            a = first_tile(jnp.where(sub == j, ua, a[:8]), a)
            inv = inv - m * rep(ui, n)
            inv = first_tile(jnp.where(sub == j, ui, inv[:8]), inv)
            for k in range(j + 1, 8):
                cs[k] = cs[k] - m * sp[k - j - 1]
        d_ref[8 * t : 8 * t + 8, :128] = a[:8]
        d_ref[8 * t : 8 * t + 8, 128:] = inv[:8]
        if t < 15:
            a, inv = a[8:], inv[8:]


def cat_store(ref, rows, chunk, hi, lo, order):
    base = 768 * chunk
    for i, w in enumerate(order):
        ref[rows, base + 256 * i : base + 256 * i + 256] = hi if w == "h" else lo


def chol(panel_ref, panel_t, m_ref, d_ref, row_buf, lt_buf, l_buf, xcat, after):
    m_ref[:, 768:] = jnp.zeros((m_ref.shape[0], 768), F32)
    m_ref[768:, :768] = jnp.zeros((m_ref.shape[0] - 768, 768), F32)
    for r in range(0, 256, 32):
        rows = [panel_t[r : r + 32, c : c + 1] for c in range(3)]
        cols = [panel_ref[c : c + 1, :] for c in range(3)]
        e = tensor_entries(rows, cols)
        for i in range(3):
            for j in range(3):
                m_ref[256 * i + r : 256 * i + r + 32, 256 * j : 256 * j + 256] = e[i, j]
    rows_at = lax.broadcasted_iota(jnp.int32, (128, 128), 0)
    cols_at = lax.broadcasted_iota(jnp.int32, (128, 128), 1)
    eye = (rows_at == cols_at).astype(F32)
    l_buf[...] = jnp.zeros(l_buf.shape, F32)
    xcat[...] = jnp.zeros(xcat.shape, BF16)
    row_buf[...] = jnp.zeros(row_buf.shape, F32)
    lt_buf[...] = jnp.zeros(lt_buf.shape, F32)
    d_ref[:, :128] = m_ref[:128, :128]
    d_ref[:, 128:] = eye

    def panel(p, _):
        base = pl.multiple_of(128 * p, 128)
        nxt = pl.multiple_of(128 * p + 128, 128)
        for i in range(5):
            at = pl.multiple_of(base + 128 * i, 128)
            m_ref[pl.ds(at, 128), pl.ds(base, 768)] -= dot3(lt_buf[128 * i : 128 * i + 128, :], row_buf[...], NN)
        factor_block(d_ref)
        x = d_ref[:, 128:]
        l_buf[pl.ds(base, 128), pl.ds(base, 128)] = jnp.where(rows_at >= cols_at, d_ref[:, :128].T, 0.0)
        row = dot3(x, m_ref[pl.ds(base, 128), pl.ds(nxt, 640)], NN)
        row_buf[:, :640] = row
        row_buf[:, 640:] = x
        m_ref[pl.ds(base, 128), pl.ds(nxt, 640)] = row
        m_ref[pl.ds(base, 128), pl.ds(768 + base, 128)] = x
        first = row[:, :128].T
        d_ref[:, :128] = m_ref[pl.ds(nxt, 128), pl.ds(nxt, 128)] - dot3(first, row[:, :128], NN)
        d_ref[:, 128:] = eye
        lt_buf[:128, :] = first
        l_buf[pl.ds(nxt, 128), pl.ds(base, 128)] = first
        for i in range(1, 5):
            lt = row[:, 128 * i : 128 * i + 128].T
            lt_buf[128 * i : 128 * i + 128, :] = lt
            l_buf[pl.ds(pl.multiple_of(nxt + 128 * i, 128), 128), pl.ds(base, 128)] = lt
        after(p)
        return 0

    lax.fori_loop(0, 6, panel, 0)
    for k in range(3):
        hi, lo = split(m_ref[256 * k : 768, 768 + 256 * k : 1024 + 256 * k])
        cat_store(xcat, slice(256 * k, 768), k, hi, lo, "hhl")


def panel_entries(rows, panel_ref, bcat):
    for r in range(0, 128, 32):
        e = tensor_entries(rows(r, 32), [panel_ref[c : c + 1, :] for c in range(3)])
        for i in range(3):
            for j in range(3):
                hi, lo = split(e[i, j])
                cat_store(bcat, slice(128 * i + r, 128 * i + r + 32), j, hi, lo, "hlh")


def panel_dot(bcat, xcat, n):
    k = 768 * (n + 1)
    return lax.dot_general(bcat[:, :k], xcat[256 * n : 256 * n + 256, :k], NT, preferred_element_type=F32)


S_HI = 256.0
S_LO = 131072.0


def split_store(v, n, row_sets, hi_ref, f8_ref, lo_ref, flip):
    hi = v.astype(BF16)
    back = hi.astype(F32)
    lo = v - back
    h8 = (back * S_HI).astype(F8)
    l8 = (lo * S_LO).astype(F8)
    for j, rows in enumerate(row_sets):
        part = slice(128 * j, 128 * j + 128)
        hi_ref[rows, 256 * n : 256 * n + 256] = hi[part]
        f8_ref[rows, 512 * n + 256 * flip : 512 * n + 256 * flip + 256] = h8[part]
        f8_ref[rows, 512 * n + 256 * (1 - flip) : 512 * n + 256 * (1 - flip) + 256] = l8[part]
        if lo_ref is not None:
            lo_ref[rows, 256 * n : 256 * n + 256] = lo[part].astype(BF16)


def lane_tile(g_ref, k, half):
    tiles = []
    for d in (4 * k + 2 * half, 4 * k + 2 * half + 1):
        tiles.append(jnp.concatenate([g_ref[d % 16, d // 16], jnp.zeros((5, 64), F32)], axis=0))
    return jnp.concatenate(tiles, axis=1)


def transposed(tile):
    return jnp.concatenate([tile, jnp.zeros((120, 128), F32)], axis=0).T


MESH = pl.DeviceIdType.MESH


def front_kernel(n_rows, n_cols, panel_ref, own_ref, l_ref, xcat, g_ref, m_ref, d_ref, row_buf, lt_buf, l_buf, pt, send_sem, recv_sem, local_sem):
    r = lax.axis_index("prow")
    c = lax.axis_index("pcol")
    local = pltpu.make_async_copy(own_ref, g_ref.at[c, r], local_sem)
    local.start()
    barrier = pltpu.get_barrier_semaphore()
    for i in range(1, n_rows):
        pl.semaphore_signal(barrier, inc=1, device_id=(lax.rem(r + i, n_rows), c), device_id_type=MESH)
    for i in range(1, n_cols):
        pl.semaphore_signal(barrier, inc=1, device_id=(r, lax.rem(c + i, n_cols)), device_id_type=MESH)

    def copy_to(src, dst, at, target):
        return pltpu.make_async_remote_copy(
            src_ref=src, dst_ref=dst, send_sem=send_sem.at[at], recv_sem=recv_sem.at[at], device_id=target, device_id_type=MESH
        )

    first = [copy_to(own_ref, g_ref.at[c, r], i, (lax.rem(r + i, n_rows), c)) for i in range(1, n_rows)]
    second = [copy_to(g_ref.at[c], g_ref.at[c], n_rows + i, (r, lax.rem(c + i, n_cols))) for i in range(1, n_cols)]

    def after(p):
        @pl.when(p == 0)
        def _():
            pl.semaphore_wait(barrier, n_rows + n_cols - 2)
            for copy in first:
                copy.start()

        @pl.when(p == 1)
        def _():
            local.wait()
            for copy in first:
                copy.wait()
            for copy in second:
                copy.start()

    for half in range(2):
        pt[128 * half : 128 * half + 128, :] = transposed(panel_ref[:, 128 * half : 128 * half + 128])
    chol(panel_ref, pt, m_ref, d_ref, row_buf, lt_buf, l_buf, xcat, after)
    l_ref[...] = l_buf[:768, :]
    for copy in second:
        copy.wait()


def front_call(panel8, own):
    n_rows, n_cols = lax.axis_size("prow"), lax.axis_size("pcol")
    vmem = pl.BlockSpec(memory_space=pltpu.VMEM)
    return pl.pallas_call(
        functools.partial(front_kernel, n_rows, n_cols),
        out_shape=[
            jax.ShapeDtypeStruct((768, 768), F32),
            jax.ShapeDtypeStruct((768, 2304), BF16),
            jax.ShapeDtypeStruct((n_cols, n_rows) + own.shape, F32),
        ],
        in_specs=[vmem, vmem],
        out_specs=[vmem, vmem, vmem],
        scratch_shapes=[
            pltpu.VMEM((1280, 1536), F32),
            pltpu.VMEM((128, 256), F32),
            pltpu.VMEM((128, 768), F32),
            pltpu.VMEM((640, 128), F32),
            pltpu.VMEM((1408, 768), F32),
            pltpu.VMEM((256, 128), F32),
            pltpu.SemaphoreType.DMA((n_rows + n_cols,)),
            pltpu.SemaphoreType.DMA((n_rows + n_cols,)),
            pltpu.SemaphoreType.DMA,
        ],
        compiler_params=pltpu.CompilerParams(collective_id=0, has_side_effects=True, vmem_limit_bytes=40 << 20),
        name="factor_and_gather",
    )(panel8, own)


def kernel(slot_ref, panel_ref, g_ref, xcat, own_ref, out_ref, chi, cf8, rhi0, rhi1, rf80, rf81, rlo, bcat, rowt, colt, colp, ids):
    step = pl.program_id(0)
    prow, pcol = ids()
    r_hi, r_f8 = (rhi0, rhi1), (rf80, rf81)

    def row_coords(tile):
        at = pl.multiple_of(tile * 128, 128)
        return lambda r, m: [rowt[pl.ds(at + r, m), k : k + 1] for k in range(3)]

    def rows_for(tile, which):
        panel_entries(row_coords(tile), panel_ref, bcat)
        for n in range(3):
            v = panel_dot(bcat, xcat, n)
            split_store(v, n, [slice(128 * j, 128 * j + 128) for j in range(3)], r_hi[which], r_f8[which], rlo, 0)

    def own_rows(tile, which):
        for h in range(3):
            piece = (pcol % 4) * 3 + h
            comp, quarter = piece // 4, piece % 4

            @pl.when((tile // 2 == pcol // 4) & (quarter // 2 == tile % 2))
            def _():
                at = pl.multiple_of(comp * 128 + (quarter % 2) * 64, 64)
                own_ref[64 * h : 64 * h + 64, :] = r_hi[which][pl.ds(at, 64), :].astype(F32) + rlo[pl.ds(at, 64), :].astype(F32)

    @pl.when(step == 0)
    def _():
        def rows_of(i, _):
            rowt[pl.ds(pl.multiple_of(i * 128, 128), 128), :] = transposed(lane_tile(g_ref, slot_ref[prow * 4 + i // 2], i % 2))
            return 0

        lax.fori_loop(0, 8, rows_of, 0)
        for i in range(4):
            tile = lane_tile(g_ref, slot_ref[pcol * 2 + i // 2], i % 2)
            colp[:, 128 * i : 128 * i + 128] = tile
            colt[128 * i : 128 * i + 128, :] = transposed(tile)

        def col_rows(i, _):
            at = pl.multiple_of(i * 128, 128)
            dst = (i // 2) * 768 + (i % 2) * 128
            panel_entries(lambda r, m: [colt[pl.ds(at + r, m), c : c + 1] for c in range(3)], panel_ref, bcat)
            for n in range(3):
                rows = [pl.ds(pl.multiple_of(dst + 256 * j, 128), 128) for j in range(3)]
                split_store(panel_dot(bcat, xcat, n), n, rows, chi, cf8, None, 1)
            return 0

        lax.fori_loop(0, 4, col_rows, 0)
        rows_for(0, 0)

    for which in range(2):
        tile = step * 2 + which
        coords = row_coords(tile)
        own_rows(tile, which)
        for c in range(2):
            for j in range(3):
                at = 768 * c + 256 * j
                v = lax.dot_general(r_hi[which][...], chi[at : at + 256, :], NT, preferred_element_type=F32)
                w = lax.dot_general(r_f8[which][...], cf8[at : at + 256, :], NT, preferred_element_type=F32)
                v = v + w * (1.0 / (S_HI * S_LO))
                out_ref[0, :, 128 * which : 128 * which + 128, at : at + 256] = v.reshape(3, 128, 256)
            for r in range(0, 128, 32):
                e = tensor_entries(coords(r, 32), [colp[k : k + 1, 256 * c : 256 * c + 256] for k in range(3)])
                for i in range(3):
                    for j in range(3):
                        dst = (0, i, slice(128 * which + r, 128 * which + r + 32), slice(768 * c + 256 * j, 768 * c + 256 * j + 256))
                        out_ref[dst] = e[i, j] - out_ref[dst]
        rows_for(jnp.minimum(tile + 1, 7), 1 - which)


def main_call(slot_block, panel8, gathered, xcat, ids):
    whole = lambda s: (0, 0)
    vmem = lambda shape, dtype: pltpu.VMEM(shape, dtype)
    own, out = pl.pallas_call(
        functools.partial(kernel, ids=ids),
        grid=(4,),
        in_specs=[
            pl.BlockSpec(memory_space=pltpu.SMEM),
            pl.BlockSpec((8, 256), whole),
            pl.BlockSpec((16, 8, 3, 64), lambda s: (0, 0, 0, 0)),
            pl.BlockSpec((768, 2304), whole),
        ],
        out_specs=[
            pl.BlockSpec((192, 768), whole),
            pl.BlockSpec((1, 3, 256, 1536), lambda s: (s, 0, 0, 0)),
        ],
        out_shape=[
            jax.ShapeDtypeStruct((192, 768), F32),
            jax.ShapeDtypeStruct((4, 3, 256, 1536), F32),
        ],
        scratch_shapes=[
            vmem((1536, 768), BF16),
            vmem((1536, 1536), F8),
            vmem((384, 768), BF16),
            vmem((384, 768), BF16),
            vmem((384, 1536), F8),
            vmem((384, 1536), F8),
            vmem((384, 768), BF16),
            vmem((384, 2304), BF16),
            vmem((1024, 128), F32),
            vmem((512, 128), F32),
            vmem((8, 512), F32),
        ],
        compiler_params=pltpu.CompilerParams(dimension_semantics=("arbitrary",), vmem_limit_bytes=40 << 20),
        name="panel_rows_and_trailing",
    )(slot_block, panel8, gathered, xcat)
    return own, out.reshape(3072, 1536)


def shards(panel_pos, trail_pos, slot_block):
    panel8 = jnp.pad(panel_pos, ((0, 5), (0, 0)))
    factor, xcat, gathered = front_call(panel8, trail_pos)
    own, trailing = main_call(slot_block, panel8, gathered, xcat, lambda: (lax.axis_index("prow"), lax.axis_index("pcol")))
    return factor, own, trailing


def solution(mesh):
    return jax.shard_map(
        shards,
        mesh=mesh,
        in_specs=(P(), P(None, ("prow", "pcol")), P()),
        out_specs=(P(), P(("prow", "pcol"), None), P("prow", "pcol")),
        check_vma=False,
    )
```

time: 564 us -> 73.9 us (0.13)
  other arithmetic: 233 us -> 0 us
  waiting for transfers between devices: 86 us -> 0 us
  matrix products: 85.9 us -> 0 us
  Pallas kernels: 0 us -> 68.6 us
  local copies, waits for them, and re-layouts: 70.9 us -> 3.43 us
  blocking collectives: 62.9 us -> 0 us
  between operations: 18.7 us -> 0.65 us
    another operation x25 -> x0, other arithmetic: 193 us -> none  [the longest x22 130 us: shards(): factor = jnp.linalg.cholesky(diag_block)]
    pallas_call x0 -> x2, Pallas kernels: none -> 68.6 us  [the longest x1 37.5 us: main_call(): pl.pallas_call(functools.partial(kernel, ids=ids), grid=(4,), in_specs=[p...]
    all_gather x1 -> x0, blocking collectives: 62.9 us -> none  [shards(): lax.all_gather(trail_pos, ('prow', 'pcol'), axis=1, tiled=True)]
    all_gather x1 -> x0, waiting for transfers between devices: 62.4 us -> none  [shards(): left_rows = lax.all_gather(own_rows, 'pcol', axis=0, tiled=True)]
    dot_general x2 -> x0, matrix products: 57 us -> none  [outer_rows(): lax.dot_general(left_rows, right_rows, (((1,), (1,)), ((), ())), precisio...]
    add x1 -> x0, local copies, waits for them, and re-layouts: 30.6 us -> none  [block_tiles(): identity[:, :, None, None, None, None] * isotropic[None, None]]
    another operation x21 -> x0, matrix products: 28.9 us -> none  [the longest x11 18.3 us: shards(): jax.scipy.linalg.solve_triangular(factor, jnp.eye(width, dtype=factor.dty...]
    psum x1 -> x0, waiting for transfers between devices: 23.6 us -> none  [from_root(): return lax.psum(kept, axis)]
  transfers between devices with their start and end apart: 2 -> 0, of which waited for: 2 -> 0; matrix products, arithmetic and copies ran while one was open for 11% -> 0% of each run, Pallas kernels for 0% -> 0%
where the time goes in v2:
time: 73.9 us; the launch traced here: 72.7 us
  Pallas kernels  68.6 us (93%)
  local copies, waits for them, and re-layouts  3.43 us (5%)
    pallas_call x1, Pallas kernels, main_call(): pl.pallas_call(functools.partial(kernel, ids=ids), grid=(4,), in_specs=[p...  37.5 us
    pallas_call x1, Pallas kernels, front_call(): pl.pallas_call(functools.partial(front_kernel, n_rows, n_cols), out_shape...  31.2 us
    unnamed x5, local copies, waits for them, and re-layouts  2.74 us

profile of v2, /device:TPU:0, one launch (start us, length us, event | category | flops | bytes accessed | tf_op | source)
XLA Modules:
  0.0 72.7 jit_solution(11397269582209710618)
XLA Ops:
  0.6 0.7 pad.4.panel_ref
  1.3 0.0 copy-start
  1.3 0.7 copy-done
  2.0 31.2 %factor_and_gather.1 = (f32[768,768]{1,0:T(8,128)S(1)}, bf16[768,2304]{1,0:T(8,128)(2,1)S(1)}, f32[16,8,3,64]{3,2,1,0:T(4,128)S(1)}) custom-call(f32[8,256]{1,0:T(8,128)S(1)} %pad.4.panel_ref, f32[3,64]{1,0:T(4,128)S(1)} %copy-done), custom_call_target="tpu_custom_call" | custom-call | tf_op jit(solution)/shard_map/factor_and_gather/pallas_call | solution.py:242
  33.2 0.0 copy-start.1
  33.2 0.6 copy-done.1
  33.9 37.5 %panel_rows_and_trailing.1 = (f32[192,768]{1,0:T(8,128)}, f32[4,3,256,1536]{3,2,1,0:T(8,128)}) custom-call(s32[32]{0:T(128)S(1)} %copy-done.1, f32[8,256]{1,0:T(8,128)S(1)} %pad.4.panel_ref, f32[16,8,3,64]{3,2,1,0:T(4,128)S(1)} %get-tuple-element.9.g_ref, bf16[768,2304]{1,0:T(8,128)(2,1)S(1)} %get-tuple-element.10.xcat), custom_call_target="tpu_custom_call" | custom-call | tf_op jit(solution)/shard_map/panel_rows_and_trailing/pallas_call | solution.py:339
  71.3 1.4 %copy.7 = f32[768,768]{1,0:T(8,128)} copy(f32[768,768]{1,0:T(8,128)S(1)} %get-tuple-element.16) | data formatting | bytes 4718592
Async XLA Ops:
  1.3 0.7 copy-start
  33.2 0.7 copy-start.1

commit v3 on v2

--- a/solution.py
+++ b/solution.py
@@ -95,9 +95,13 @@
         ref[rows, base + 256 * i : base + 256 * i + 256] = hi if w == "h" else lo
 
 
+def pre_split_dot(a, b, dims):
+    d = functools.partial(lax.dot_general, dimension_numbers=dims, preferred_element_type=F32)
+    return d(a[0], b[0]) + (d(a[1], b[0]) + d(a[0], b[1]))
+
+
 def chol(panel_ref, panel_t, m_ref, d_ref, row_buf, lt_buf, l_buf, xcat, after):
-    m_ref[:, 768:] = jnp.zeros((m_ref.shape[0], 768), F32)
-    m_ref[768:, :768] = jnp.zeros((m_ref.shape[0] - 768, 768), F32)
+    m_ref[:768, 768:] = jnp.zeros((768, 768), F32)
     for r in range(0, 256, 32):
         rows = [panel_t[r : r + 32, c : c + 1] for c in range(3)]
         cols = [panel_ref[c : c + 1, :] for c in range(3)]
@@ -147,39 +151,6 @@
         cat_store(xcat, slice(256 * k, 768), k, hi, lo, "hhl")
 
 
-def panel_entries(rows, panel_ref, bcat):
-    for r in range(0, 128, 32):
-        e = tensor_entries(rows(r, 32), [panel_ref[c : c + 1, :] for c in range(3)])
-        for i in range(3):
-            for j in range(3):
-                hi, lo = split(e[i, j])
-                cat_store(bcat, slice(128 * i + r, 128 * i + r + 32), j, hi, lo, "hlh")
-
-
-def panel_dot(bcat, xcat, n):
-    k = 768 * (n + 1)
-    return lax.dot_general(bcat[:, :k], xcat[256 * n : 256 * n + 256, :k], NT, preferred_element_type=F32)
-
-
-S_HI = 256.0
-S_LO = 131072.0
-
-
-def split_store(v, n, row_sets, hi_ref, f8_ref, lo_ref, flip):
-    hi = v.astype(BF16)
-    back = hi.astype(F32)
-    lo = v - back
-    h8 = (back * S_HI).astype(F8)
-    l8 = (lo * S_LO).astype(F8)
-    for j, rows in enumerate(row_sets):
-        part = slice(128 * j, 128 * j + 128)
-        hi_ref[rows, 256 * n : 256 * n + 256] = hi[part]
-        f8_ref[rows, 512 * n + 256 * flip : 512 * n + 256 * flip + 256] = h8[part]
-        f8_ref[rows, 512 * n + 256 * (1 - flip) : 512 * n + 256 * (1 - flip) + 256] = l8[part]
-        if lo_ref is not None:
-            lo_ref[rows, 256 * n : 256 * n + 256] = lo[part].astype(BF16)
-
-
 def lane_tile(g_ref, k, half):
     tiles = []
     for d in (4 * k + 2 * half, 4 * k + 2 * half + 1):
@@ -194,7 +165,7 @@
 MESH = pl.DeviceIdType.MESH
 
 
-def front_kernel(n_rows, n_cols, panel_ref, own_ref, l_ref, xcat, g_ref, m_ref, d_ref, row_buf, lt_buf, l_buf, pt, send_sem, recv_sem, local_sem):
+def front_kernel(n_rows, n_cols, panel_ref, own_ref, l_ref, xcat, g_ref, m_ref, d_ref, row_buf, lt_buf, l_buf, p8, pt, send_sem, recv_sem, local_sem):
     r = lax.axis_index("prow")
     c = lax.axis_index("pcol")
     local = pltpu.make_async_copy(own_ref, g_ref.at[c, r], local_sem)
@@ -228,15 +199,17 @@
             for copy in second:
                 copy.start()
 
+    p8[...] = jnp.zeros((8, 256), F32)
+    p8[:3, :] = panel_ref[...]
     for half in range(2):
-        pt[128 * half : 128 * half + 128, :] = transposed(panel_ref[:, 128 * half : 128 * half + 128])
+        pt[128 * half : 128 * half + 128, :] = transposed(p8[:, 128 * half : 128 * half + 128])
     chol(panel_ref, pt, m_ref, d_ref, row_buf, lt_buf, l_buf, xcat, after)
     l_ref[...] = l_buf[:768, :]
     for copy in second:
         copy.wait()
 
 
-def front_call(panel8, own):
+def front_call(panel_pos, own):
     n_rows, n_cols = lax.axis_size("prow"), lax.axis_size("pcol")
     vmem = pl.BlockSpec(memory_space=pltpu.VMEM)
     return pl.pallas_call(
@@ -246,14 +219,16 @@
             jax.ShapeDtypeStruct((768, 2304), BF16),
             jax.ShapeDtypeStruct((n_cols, n_rows) + own.shape, F32),
         ],
-        in_specs=[vmem, vmem],
+        in_specs=[vmem, pl.BlockSpec(memory_space=pl.ANY)],
         out_specs=[vmem, vmem, vmem],
+        cost_estimate=pl.CostEstimate(flops=10**10, bytes_accessed=10**7, transcendentals=0),
         scratch_shapes=[
             pltpu.VMEM((1280, 1536), F32),
             pltpu.VMEM((128, 256), F32),
             pltpu.VMEM((128, 768), F32),
             pltpu.VMEM((640, 128), F32),
             pltpu.VMEM((1408, 768), F32),
+            pltpu.VMEM((8, 256), F32),
             pltpu.VMEM((256, 128), F32),
             pltpu.SemaphoreType.DMA((n_rows + n_cols,)),
             pltpu.SemaphoreType.DMA((n_rows + n_cols,)),
@@ -261,36 +236,100 @@
         ],
         compiler_params=pltpu.CompilerParams(collective_id=0, has_side_effects=True, vmem_limit_bytes=40 << 20),
         name="factor_and_gather",
-    )(panel8, own)
-
-
-def kernel(slot_ref, panel_ref, g_ref, xcat, own_ref, out_ref, chi, cf8, rhi0, rhi1, rf80, rf81, rlo, bcat, rowt, colt, colp, ids):
+    )(panel_pos, own)
+
+
+def panel_entries(rows, panel_ref, bcat):
+    for r in range(0, 128, 32):
+        e = tensor_entries(rows(r, 32), [panel_ref[c : c + 1, :] for c in range(3)])
+        for i in range(3):
+            for j in range(3):
+                hi, lo = split(e[i, j])
+                cat_store(bcat, slice(128 * i + r, 128 * i + r + 32), j, hi, lo, "hlh")
+
+
+ROW = (2048.0, 256.0, 131072.0)
+COL = (1024.0, 16.0, 8192.0)
+BACK = 1.0 / (2048.0 * 1024.0)
+F8_MAX = 448.0
+
+
+def parts_of(v, scales):
+    scaled = v * scales[0]
+    hi = scaled.astype(BF16)
+    rest = scaled - hi.astype(F32)
+    return hi, scaled * (scales[1] / scales[0]), rest * (scales[2] / scales[0])
+
+
+def row_parts(rows, panel_ref, hi_ref, f8_ref):
+    for r in range(0, 128, 32):
+        e = tensor_entries(rows(r, 32), [panel_ref[c : c + 1, :] for c in range(3)])
+        parts = {(i, j): parts_of(e[i, j], ROW) for i in range(3) for j in range(i, 3)}
+        for i in range(3):
+            at = slice(128 * i + r, 128 * i + r + 32)
+            for j in range(3):
+                hi, whole, rest = parts[min(i, j), max(i, j)]
+                hi_ref[at, 256 * j : 256 * j + 256] = hi
+                f8_ref[at, 512 * j : 512 * j + 256] = whole.astype(F8)
+                f8_ref[at, 512 * j + 256 : 512 * j + 512] = rest.astype(F8)
+
+
+def col_store(v, dst, chi, cf8):
+    for n in range(3):
+        hi, whole, rest = parts_of(v[:, 256 * n : 256 * n + 256], COL)
+        whole = jnp.clip(whole, -F8_MAX, F8_MAX).astype(F8)
+        rest = jnp.clip(rest, -F8_MAX, F8_MAX).astype(F8)
+        for j in range(3):
+            rows, part = slice(dst + 256 * j, dst + 256 * j + 128), slice(128 * j, 128 * j + 128)
+            chi[rows, 256 * n : 256 * n + 256] = hi[part]
+            cf8[rows, 512 * n : 512 * n + 256] = rest[part]
+            cf8[rows, 512 * n + 256 : 512 * n + 512] = whole[part]
+
+
+def kernel(slot_ref, panel_ref, g_ref, xcat, l_in, l_out, own_ref, out_ref, wcat, chi, cf8, rhi, rf8, bcat, ocat, rowt, colt, colp, l_sem, ids):
     step = pl.program_id(0)
     prow, pcol = ids()
-    r_hi, r_f8 = (rhi0, rhi1), (rf80, rf81)
+    l_copy = pltpu.make_async_copy(l_in, l_out, l_sem)
+    panel_cols = lambda: [panel_ref[c : c + 1, :] for c in range(3)]
 
     def row_coords(tile):
         at = pl.multiple_of(tile * 128, 128)
         return lambda r, m: [rowt[pl.ds(at + r, m), k : k + 1] for k in range(3)]
 
-    def rows_for(tile, which):
-        panel_entries(row_coords(tile), panel_ref, bcat)
-        for n in range(3):
-            v = panel_dot(bcat, xcat, n)
-            split_store(v, n, [slice(128 * j, 128 * j + 128) for j in range(3)], r_hi[which], r_f8[which], rlo, 0)
-
-    def own_rows(tile, which):
+    def inverse_of_diag():
+        for b in range(3):
+            for a in range(3):
+                k = slice(256 * max(a, b), 768)
+                hi = lambda q: xcat[k, 768 * q : 768 * q + 256]
+                lo = lambda q: xcat[k, 768 * q + 512 : 768 * q + 768]
+                w = pre_split_dot((hi(a), lo(a)), (hi(b), lo(b)), TN)
+                wh, wl = split(w)
+                at = slice(256 * b, 256 * b + 256)
+                wcat[768 * a : 768 * a + 256, at] = wh
+                wcat[768 * a + 256 : 768 * a + 512, at] = wh
+                wcat[768 * a + 512 : 768 * a + 768, at] = wl
+
+    def own_rows():
         for h in range(3):
             piece = (pcol % 4) * 3 + h
             comp, quarter = piece // 4, piece % 4
-
-            @pl.when((tile // 2 == pcol // 4) & (quarter // 2 == tile % 2))
-            def _():
-                at = pl.multiple_of(comp * 128 + (quarter % 2) * 64, 64)
-                own_ref[64 * h : 64 * h + 64, :] = r_hi[which][pl.ds(at, 64), :].astype(F32) + rlo[pl.ds(at, 64), :].astype(F32)
+            at = pl.multiple_of((pcol // 4) * 256 + quarter * 64, 64)
+            for r in range(0, 64, 32):
+                diff, iso, directed = pair_terms([rowt[pl.ds(at + r, 32), k : k + 1] for k in range(3)], panel_cols())
+                g = directed * jnp.where(comp == 0, diff[0], jnp.where(comp == 1, diff[1], diff[2]))
+                for j in range(3):
+                    hi, lo = split(g * diff[j] + jnp.where(comp == j, iso, 0.0))
+                    cat_store(ocat, slice(64 * h + r, 64 * h + r + 32), j, hi, lo, "hlh")
+        for n in range(3):
+            k = 768 * (n + 1)
+            own_ref[:, 256 * n : 256 * n + 256] = lax.dot_general(
+                ocat[:, :k], xcat[256 * n : 256 * n + 256, :k], NT, preferred_element_type=F32
+            )
 
     @pl.when(step == 0)
     def _():
+        l_copy.start()
+
         def rows_of(i, _):
             rowt[pl.ds(pl.multiple_of(i * 128, 128), 128), :] = transposed(lane_tile(g_ref, slot_ref[prow * 4 + i // 2], i % 2))
             return 0
@@ -300,83 +339,89 @@
             tile = lane_tile(g_ref, slot_ref[pcol * 2 + i // 2], i % 2)
             colp[:, 128 * i : 128 * i + 128] = tile
             colt[128 * i : 128 * i + 128, :] = transposed(tile)
-
-        def col_rows(i, _):
-            at = pl.multiple_of(i * 128, 128)
-            dst = (i // 2) * 768 + (i % 2) * 128
-            panel_entries(lambda r, m: [colt[pl.ds(at + r, m), c : c + 1] for c in range(3)], panel_ref, bcat)
-            for n in range(3):
-                rows = [pl.ds(pl.multiple_of(dst + 256 * j, 128), 128) for j in range(3)]
-                split_store(panel_dot(bcat, xcat, n), n, rows, chi, cf8, None, 1)
-            return 0
-
-        lax.fori_loop(0, 4, col_rows, 0)
-        rows_for(0, 0)
-
-    for which in range(2):
-        tile = step * 2 + which
-        coords = row_coords(tile)
-        own_rows(tile, which)
-        for c in range(2):
-            for j in range(3):
-                at = 768 * c + 256 * j
-                v = lax.dot_general(r_hi[which][...], chi[at : at + 256, :], NT, preferred_element_type=F32)
-                w = lax.dot_general(r_f8[which][...], cf8[at : at + 256, :], NT, preferred_element_type=F32)
-                v = v + w * (1.0 / (S_HI * S_LO))
-                out_ref[0, :, 128 * which : 128 * which + 128, at : at + 256] = v.reshape(3, 128, 256)
-            for r in range(0, 128, 32):
-                e = tensor_entries(coords(r, 32), [colp[k : k + 1, 256 * c : 256 * c + 256] for k in range(3)])
-                for i in range(3):
-                    for j in range(3):
-                        dst = (0, i, slice(128 * which + r, 128 * which + r + 32), slice(768 * c + 256 * j, 768 * c + 256 * j + 256))
-                        out_ref[dst] = e[i, j] - out_ref[dst]
-        rows_for(jnp.minimum(tile + 1, 7), 1 - which)
-
-
-def main_call(slot_block, panel8, gathered, xcat, ids):
+        inverse_of_diag()
+        for i in range(4):
+            buf = bcat.at[i % 2]
+            panel_entries(lambda r, m: [colt[128 * i + r : 128 * i + r + m, c : c + 1] for c in range(3)], panel_ref, buf)
+            v = lax.dot_general(buf[...], wcat[...], NN, preferred_element_type=F32)
+            col_store(v, (i // 2) * 768 + (i % 2) * 128, chi, cf8)
+        own_rows()
+        row_parts(row_coords(0), panel_ref, rhi.at[0], rf8.at[0])
+
+    which = step % 2
+    coords = row_coords(step)
+
+    def trailing(c):
+        at = 768 * c
+        v = lax.dot_general(rhi[which], chi[at : at + 768, :], NT, preferred_element_type=F32)
+        v = v + lax.dot_general(rf8[which], cf8[at : at + 768, :], NT, preferred_element_type=F32)
+        out_ref[0, :, :, at : at + 768] = v.reshape(3, 128, 768)
+        for r in range(0, 128, 32):
+            e = tensor_entries(coords(r, 32), [colp[k : k + 1, 256 * c : 256 * c + 256] for k in range(3)])
+            for i in range(3):
+                for j in range(3):
+                    dst = (0, i, slice(r, r + 32), slice(768 * c + 256 * j, 768 * c + 256 * j + 256))
+                    out_ref[dst] = e[i, j] - out_ref[dst] * BACK
+
+    @pl.when(step < 7)
+    def _():
+        trailing(0)
+        row_parts(row_coords(step + 1), panel_ref, rhi.at[1 - which], rf8.at[1 - which])
+        trailing(1)
+
+    @pl.when(step == 7)
+    def _():
+        trailing(0)
+        trailing(1)
+        l_copy.wait()
+
+
+def main_call(slot_block, panel_pos, gathered, xcat, factor, ids):
     whole = lambda s: (0, 0)
     vmem = lambda shape, dtype: pltpu.VMEM(shape, dtype)
-    own, out = pl.pallas_call(
+    l, own, out = pl.pallas_call(
         functools.partial(kernel, ids=ids),
-        grid=(4,),
+        grid=(8,),
         in_specs=[
             pl.BlockSpec(memory_space=pltpu.SMEM),
-            pl.BlockSpec((8, 256), whole),
+            pl.BlockSpec((3, 256), whole),
             pl.BlockSpec((16, 8, 3, 64), lambda s: (0, 0, 0, 0)),
             pl.BlockSpec((768, 2304), whole),
+            pl.BlockSpec(memory_space=pltpu.VMEM),
         ],
         out_specs=[
+            pl.BlockSpec(memory_space=pl.ANY),
             pl.BlockSpec((192, 768), whole),
-            pl.BlockSpec((1, 3, 256, 1536), lambda s: (s, 0, 0, 0)),
+            pl.BlockSpec((1, 3, 128, 1536), lambda s: (s // 2, 0, s % 2, 0)),
         ],
         out_shape=[
+            jax.ShapeDtypeStruct((768, 768), F32),
             jax.ShapeDtypeStruct((192, 768), F32),
             jax.ShapeDtypeStruct((4, 3, 256, 1536), F32),
         ],
         scratch_shapes=[
+            vmem((2304, 768), BF16),
             vmem((1536, 768), BF16),
             vmem((1536, 1536), F8),
-            vmem((384, 768), BF16),
-            vmem((384, 768), BF16),
-            vmem((384, 1536), F8),
-            vmem((384, 1536), F8),
-            vmem((384, 768), BF16),
-            vmem((384, 2304), BF16),
+            vmem((2, 384, 768), BF16),
+            vmem((2, 384, 1536), F8),
+            vmem((2, 384, 2304), BF16),
+            vmem((192, 2304), BF16),
             vmem((1024, 128), F32),
             vmem((512, 128), F32),
             vmem((8, 512), F32),
+            pltpu.SemaphoreType.DMA,
         ],
         compiler_params=pltpu.CompilerParams(dimension_semantics=("arbitrary",), vmem_limit_bytes=40 << 20),
+        cost_estimate=pl.CostEstimate(flops=3 * 10**10, bytes_accessed=3 * 10**7, transcendentals=0),
         name="panel_rows_and_trailing",
-    )(slot_block, panel8, gathered, xcat)
-    return own, out.reshape(3072, 1536)
+    )(slot_block, panel_pos, gathered, xcat, factor)
+    return l, own, out.reshape(3072, 1536)
 
 
 def shards(panel_pos, trail_pos, slot_block):
-    panel8 = jnp.pad(panel_pos, ((0, 5), (0, 0)))
-    factor, xcat, gathered = front_call(panel8, trail_pos)
-    own, trailing = main_call(slot_block, panel8, gathered, xcat, lambda: (lax.axis_index("prow"), lax.axis_index("pcol")))
-    return factor, own, trailing
+    factor, xcat, gathered = front_call(panel_pos, trail_pos)
+    return main_call(slot_block, panel_pos, gathered, xcat, factor, lambda: (lax.axis_index("prow"), lax.axis_index("pcol")))
 
 
 def solution(mesh):

time: 73.9 us -> 66.8 us (0.904)
  Pallas kernels: 68.6 us -> 63.4 us
  local copies, waits for them, and re-layouts: 3.43 us -> 1.36 us
    pallas_call x1, Pallas kernels: 37.5 us -> 32.3 us  [main_call(): pl.pallas_call(functools.partial(kernel, ids=ids), grid=(8,), in_specs=[p...]
    unnamed x5 -> x6, local copies, waits for them, and re-layouts: 2.74 us -> 1.36 us
where the time goes in v3:
time: 66.8 us; the launch traced here: 65.6 us
  Pallas kernels  63.4 us (95%)
  local copies, waits for them, and re-layouts  1.36 us (2%)
  between operations  0.82 us (1%)
    pallas_call x1, Pallas kernels, main_call(): pl.pallas_call(functools.partial(kernel, ids=ids), grid=(8,), in_specs=[p...  32.3 us
    pallas_call x1, Pallas kernels, front_call(): pl.pallas_call(functools.partial(front_kernel, n_rows, n_cols), out_shape...  31.1 us
    unnamed x6, local copies, waits for them, and re-layouts  1.36 us

profile of v3, /device:TPU:0, one launch (start us, length us, event | category | flops | bytes accessed | tf_op | source)
XLA Modules:
  0.0 65.6 jit_solution(8627718482484417815)
XLA Ops:
  0.6 0.0 copy-start
  0.6 0.7 %copy-done = f32[3,256]{1,0:T(4,128)S(1)} copy-done((f32[3,256]{1,0:T(4,128)S(1)}, f32[3,256]{1,0:T(4,128)}, u32[]{:S(2)}) %copy-start) | copy-done | bytes 3096
  1.3 0.0 copy-start.1
  1.3 0.7 %copy-done.1 = f32[3,64]{1,0:T(4,128)S(1)} copy-done((f32[3,64]{1,0:T(4,128)S(1)}, f32[3,64]{1,0:T(4,128)}, u32[]{:S(2)}) %copy-start.1) | copy-done | bytes 792
  2.0 0.0 copy-start.2
  2.0 31.1 %factor_and_gather.1 = (f32[768,768]{1,0:T(8,128)S(1)}, bf16[768,2304]{1,0:T(8,128)(2,1)S(1)}, f32[16,8,3,64]{3,2,1,0:T(4,128)S(1)}) custom-call(f32[3,256]{1,0:T(4,128)S(1)} %copy-done, f32[3,64]{1,0:T(4,128)S(1)} %copy-done.1), custom_call_target="tpu_custom_call" | custom-call | flops 10000000000 | bytes 10000000 | tf_op jit(solution)/shard_map/factor_and_gather/pallas_call | solution.py:215
  33.1 0.0 copy-done.2
  33.2 32.3 %panel_rows_and_trailing.1 = (f32[768,768]{1,0:T(8,128)}, f32[192,768]{1,0:T(8,128)}, f32[4,3,256,1536]{3,2,1,0:T(8,128)}) custom-call(s32[32]{0:T(128)S(1)} %copy-done.2, f32[3,256]{1,0:T(4,128)S(1)} %copy-done, f32[16,8,3,64]{3,2,1,0:T(4,128)S(1)} %get-tuple-element.9.g_ref, bf16[768,2304]{1,0:T(8,128)(2,1)S(1)} %get-tuple-element.10.xcat, ...), custom_call_target="tpu_custom_call" | custom-call | flops 30000001024 | bytes 30000000 | tf_op jit(solution)/shard_map/panel_rows_and_trailing/pallas_call | solution.py:382
Async XLA Ops:
  0.6 0.7 %copy-start = (f32[3,256]{1,0:T(4,128)S(1)}, f32[3,256]{1,0:T(4,128)}, u32[]{:S(2)}) copy-start(f32[3,256]{1,0:T(4,128)} %panel_ref.3) | copy-start | bytes 9220
  1.3 0.7 %copy-start.1 = (f32[3,64]{1,0:T(4,128)S(1)}, f32[3,64]{1,0:T(4,128)}, u32[]{:S(2)}) copy-start(f32[3,64]{1,0:T(4,128)} %own_ref.1) | copy-start | bytes 2308
  2.0 31.1 %copy-start.2 = (s32[32]{0:T(128)S(1)}, s32[32]{0:T(128)}, u32[]{:S(2)}) copy-start(s32[32]{0:T(128)} %slot_ref.1) | copy-start | bytes 388

commit v4 on v3

--- a/solution.py
+++ b/solution.py
@@ -101,7 +101,7 @@
 
 
 def chol(panel_ref, panel_t, m_ref, d_ref, row_buf, lt_buf, l_buf, xcat, after):
-    m_ref[:768, 768:] = jnp.zeros((768, 768), F32)
+    m_ref[128:768, 768:1408] = jnp.zeros((640, 640), F32)
     for r in range(0, 256, 32):
         rows = [panel_t[r : r + 32, c : c + 1] for c in range(3)]
         cols = [panel_ref[c : c + 1, :] for c in range(3)]
@@ -112,8 +112,6 @@
     rows_at = lax.broadcasted_iota(jnp.int32, (128, 128), 0)
     cols_at = lax.broadcasted_iota(jnp.int32, (128, 128), 1)
     eye = (rows_at == cols_at).astype(F32)
-    l_buf[...] = jnp.zeros(l_buf.shape, F32)
-    xcat[...] = jnp.zeros(xcat.shape, BF16)
     row_buf[...] = jnp.zeros(row_buf.shape, F32)
     lt_buf[...] = jnp.zeros(lt_buf.shape, F32)
     d_ref[:, :128] = m_ref[:128, :128]
@@ -122,9 +120,11 @@
     def panel(p, _):
         base = pl.multiple_of(128 * p, 128)
         nxt = pl.multiple_of(128 * p + 128, 128)
+        row_parts = split(row_buf[...])
         for i in range(5):
             at = pl.multiple_of(base + 128 * i, 128)
-            m_ref[pl.ds(at, 128), pl.ds(base, 768)] -= dot3(lt_buf[128 * i : 128 * i + 128, :], row_buf[...], NN)
+            lt_parts = split(lt_buf[128 * i : 128 * i + 128, :])
+            m_ref[pl.ds(at, 128), pl.ds(base, 768)] -= pre_split_dot(lt_parts, row_parts, NN)
         factor_block(d_ref)
         x = d_ref[:, 128:]
         l_buf[pl.ds(base, 128), pl.ds(base, 128)] = jnp.where(rows_at >= cols_at, d_ref[:, :128].T, 0.0)
@@ -146,9 +146,23 @@
         return 0
 
     lax.fori_loop(0, 6, panel, 0)
-    for k in range(3):
-        hi, lo = split(m_ref[256 * k : 768, 768 + 256 * k : 1024 + 256 * k])
-        cat_store(xcat, slice(256 * k, 768), k, hi, lo, "hhl")
+    for q in range(6):
+        rows = slice(128 * q, 128 * q + 128)
+        for c in range(6):
+            zero = jnp.zeros((128, 128), BF16)
+            hi, lo = (zero, zero) if c > q else split(m_ref[rows, 768 + 128 * c : 896 + 128 * c])
+            at = 768 * (c // 2) + 128 * (c % 2)
+            xcat[rows, at : at + 128] = hi
+            xcat[rows, at + 256 : at + 384] = hi
+            xcat[rows, at + 512 : at + 640] = lo
+
+
+def store_factor(l_ref, l_buf):
+    for q in range(6):
+        rows = slice(128 * q, 128 * q + 128)
+        l_ref[rows, : 128 * q + 128] = l_buf[rows, : 128 * q + 128]
+        if q < 5:
+            l_ref[rows, 128 * q + 128 :] = jnp.zeros((128, 640 - 128 * q), F32)
 
 
 def lane_tile(g_ref, k, half):
@@ -165,11 +179,13 @@
 MESH = pl.DeviceIdType.MESH
 
 
-def front_kernel(n_rows, n_cols, panel_ref, own_ref, l_ref, xcat, g_ref, m_ref, d_ref, row_buf, lt_buf, l_buf, p8, pt, send_sem, recv_sem, local_sem):
+def front_kernel(n_rows, n_cols, panel_ref, own_ref, l_ref, xcat, g_ref, p8, m_ref, d_ref, row_buf, lt_buf, l_buf, p3, pt, send_sem, recv_sem, local_sem, panel_sem):
     r = lax.axis_index("prow")
     c = lax.axis_index("pcol")
     local = pltpu.make_async_copy(own_ref, g_ref.at[c, r], local_sem)
     local.start()
+    panel_copy = pltpu.make_async_copy(panel_ref, p3, panel_sem)
+    panel_copy.start()
     barrier = pltpu.get_barrier_semaphore()
     for i in range(1, n_rows):
         pl.semaphore_signal(barrier, inc=1, device_id=(lax.rem(r + i, n_rows), c), device_id_type=MESH)
@@ -200,11 +216,12 @@
                 copy.start()
 
     p8[...] = jnp.zeros((8, 256), F32)
-    p8[:3, :] = panel_ref[...]
+    panel_copy.wait()
+    p8[:3, :] = p3[...]
     for half in range(2):
         pt[128 * half : 128 * half + 128, :] = transposed(p8[:, 128 * half : 128 * half + 128])
-    chol(panel_ref, pt, m_ref, d_ref, row_buf, lt_buf, l_buf, xcat, after)
-    l_ref[...] = l_buf[:768, :]
+    chol(p8, pt, m_ref, d_ref, row_buf, lt_buf, l_buf, xcat, after)
+    store_factor(l_ref, l_buf)
     for copy in second:
         copy.wait()
 
@@ -218,9 +235,10 @@
             jax.ShapeDtypeStruct((768, 768), F32),
             jax.ShapeDtypeStruct((768, 2304), BF16),
             jax.ShapeDtypeStruct((n_cols, n_rows) + own.shape, F32),
+            jax.ShapeDtypeStruct((8, 256), F32),
         ],
-        in_specs=[vmem, pl.BlockSpec(memory_space=pl.ANY)],
-        out_specs=[vmem, vmem, vmem],
+        in_specs=[pl.BlockSpec(memory_space=pltpu.HBM)] * 2,
+        out_specs=[vmem] * 4,
         cost_estimate=pl.CostEstimate(flops=10**10, bytes_accessed=10**7, transcendentals=0),
         scratch_shapes=[
             pltpu.VMEM((1280, 1536), F32),
@@ -228,10 +246,11 @@
             pltpu.VMEM((128, 768), F32),
             pltpu.VMEM((640, 128), F32),
             pltpu.VMEM((1408, 768), F32),
-            pltpu.VMEM((8, 256), F32),
+            pltpu.VMEM((3, 256), F32),
             pltpu.VMEM((256, 128), F32),
             pltpu.SemaphoreType.DMA((n_rows + n_cols,)),
             pltpu.SemaphoreType.DMA((n_rows + n_cols,)),
+            pltpu.SemaphoreType.DMA,
             pltpu.SemaphoreType.DMA,
         ],
         compiler_params=pltpu.CompilerParams(collective_id=0, has_side_effects=True, vmem_limit_bytes=40 << 20),
@@ -286,10 +305,16 @@
             cf8[rows, 512 * n + 256 : 512 * n + 512] = whole[part]
 
 
-def kernel(slot_ref, panel_ref, g_ref, xcat, l_in, l_out, own_ref, out_ref, wcat, chi, cf8, rhi, rf8, bcat, ocat, rowt, colt, colp, l_sem, ids):
-    step = pl.program_id(0)
+def kernel(slot_ref, panel_ref, g_ref, xcat, l_in, l_out, own_out, out_ref, own_ref, wcat, chi, cf8, rhi0, rhi1, rf80, rf81, bcat, ocat, rowt, colt, colp, obuf, l_sem, own_sem, o_sem, ids):
     prow, pcol = ids()
     l_copy = pltpu.make_async_copy(l_in, l_out, l_sem)
+    own_copy = pltpu.make_async_copy(own_ref, own_out, own_sem)
+    l_copy.start()
+
+    def out_copy(at_step, half):
+        rows = pl.ds(128 * half, 128)
+        return pltpu.make_async_copy(obuf.at[at_step % 2, half], out_ref.at[at_step, :, rows, :], o_sem.at[at_step % 2, half])
+
     panel_cols = lambda: [panel_ref[c : c + 1, :] for c in range(3)]
 
     def row_coords(tile):
@@ -326,93 +351,97 @@
                 ocat[:, :k], xcat[256 * n : 256 * n + 256, :k], NT, preferred_element_type=F32
             )
 
-    @pl.when(step == 0)
-    def _():
-        l_copy.start()
-
-        def rows_of(i, _):
-            rowt[pl.ds(pl.multiple_of(i * 128, 128), 128), :] = transposed(lane_tile(g_ref, slot_ref[prow * 4 + i // 2], i % 2))
-            return 0
-
-        lax.fori_loop(0, 8, rows_of, 0)
-        for i in range(4):
-            tile = lane_tile(g_ref, slot_ref[pcol * 2 + i // 2], i % 2)
-            colp[:, 128 * i : 128 * i + 128] = tile
-            colt[128 * i : 128 * i + 128, :] = transposed(tile)
-        inverse_of_diag()
-        for i in range(4):
-            buf = bcat.at[i % 2]
-            panel_entries(lambda r, m: [colt[128 * i + r : 128 * i + r + m, c : c + 1] for c in range(3)], panel_ref, buf)
-            v = lax.dot_general(buf[...], wcat[...], NN, preferred_element_type=F32)
-            col_store(v, (i // 2) * 768 + (i % 2) * 128, chi, cf8)
-        own_rows()
-        row_parts(row_coords(0), panel_ref, rhi.at[0], rf8.at[0])
-
-    which = step % 2
-    coords = row_coords(step)
-
-    def trailing(c):
+    def rows_of(i, _):
+        rowt[pl.ds(pl.multiple_of(i * 128, 128), 128), :] = transposed(lane_tile(g_ref, slot_ref[prow * 4 + i // 2], i % 2))
+        return 0
+
+    lax.fori_loop(0, 8, rows_of, 0)
+    for i in range(4):
+        tile = lane_tile(g_ref, slot_ref[pcol * 2 + i // 2], i % 2)
+        colp[:, 128 * i : 128 * i + 128] = tile
+        colt[128 * i : 128 * i + 128, :] = transposed(tile)
+    inverse_of_diag()
+    for i in range(4):
+        buf = bcat.at[i % 2]
+        panel_entries(lambda r, m: [colt[128 * i + r : 128 * i + r + m, c : c + 1] for c in range(3)], panel_ref, buf)
+        v = lax.dot_general(buf[...], wcat[...], NN, preferred_element_type=F32)
+        col_store(v, (i // 2) * 768 + (i % 2) * 128, chi, cf8)
+    own_rows()
+    own_copy.start()
+    row_parts(row_coords(0), panel_ref, rhi0, rf80)
+
+    def trailing(step, slot, which, c):
+        coords = row_coords(2 * step + which)
         at = 768 * c
-        v = lax.dot_general(rhi[which], chi[at : at + 768, :], NT, preferred_element_type=F32)
-        v = v + lax.dot_general(rf8[which], cf8[at : at + 768, :], NT, preferred_element_type=F32)
-        out_ref[0, :, :, at : at + 768] = v.reshape(3, 128, 768)
+        v = lax.dot_general((rhi0, rhi1)[which][...], chi[at : at + 768, :], NT, preferred_element_type=F32)
+        v = v + lax.dot_general((rf80, rf81)[which][...], cf8[at : at + 768, :], NT, preferred_element_type=F32)
+        obuf[slot, which, :, :, at : at + 768] = v.reshape(3, 128, 768)
         for r in range(0, 128, 32):
             e = tensor_entries(coords(r, 32), [colp[k : k + 1, 256 * c : 256 * c + 256] for k in range(3)])
             for i in range(3):
                 for j in range(3):
-                    dst = (0, i, slice(r, r + 32), slice(768 * c + 256 * j, 768 * c + 256 * j + 256))
-                    out_ref[dst] = e[i, j] - out_ref[dst] * BACK
-
-    @pl.when(step < 7)
-    def _():
-        trailing(0)
-        row_parts(row_coords(step + 1), panel_ref, rhi.at[1 - which], rf8.at[1 - which])
-        trailing(1)
-
-    @pl.when(step == 7)
-    def _():
-        trailing(0)
-        trailing(1)
-        l_copy.wait()
+                    dst = (slot, which, i, slice(r, r + 32), slice(768 * c + 256 * j, 768 * c + 256 * j + 256))
+                    obuf[dst] = e[i, j] - obuf[dst] * BACK
+
+    def two_tiles(step, _):
+        slot = step % 2
+
+        @pl.when(step >= 2)
+        def _():
+            for half in range(2):
+                out_copy(step - 2, half).wait()
+
+        trailing(step, slot, 0, 0)
+        row_parts(row_coords(2 * step + 1), panel_ref, rhi1, rf81)
+        trailing(step, slot, 0, 1)
+        out_copy(step, 0).start()
+        trailing(step, slot, 1, 0)
+        row_parts(row_coords(jnp.minimum(2 * step + 2, 7)), panel_ref, rhi0, rf80)
+        trailing(step, slot, 1, 1)
+        out_copy(step, 1).start()
+        return 0
+
+    lax.fori_loop(0, 4, two_tiles, 0)
+    for step in (2, 3):
+        for half in range(2):
+            out_copy(step, half).wait()
+    own_copy.wait()
+    l_copy.wait()
 
 
 def main_call(slot_block, panel_pos, gathered, xcat, factor, ids):
-    whole = lambda s: (0, 0)
+    whole = pl.BlockSpec(memory_space=pltpu.VMEM)
+    anywhere = pl.BlockSpec(memory_space=pl.ANY)
     vmem = lambda shape, dtype: pltpu.VMEM(shape, dtype)
     l, own, out = pl.pallas_call(
         functools.partial(kernel, ids=ids),
-        grid=(8,),
-        in_specs=[
-            pl.BlockSpec(memory_space=pltpu.SMEM),
-            pl.BlockSpec((3, 256), whole),
-            pl.BlockSpec((16, 8, 3, 64), lambda s: (0, 0, 0, 0)),
-            pl.BlockSpec((768, 2304), whole),
-            pl.BlockSpec(memory_space=pltpu.VMEM),
-        ],
-        out_specs=[
-            pl.BlockSpec(memory_space=pl.ANY),
-            pl.BlockSpec((192, 768), whole),
-            pl.BlockSpec((1, 3, 128, 1536), lambda s: (s // 2, 0, s % 2, 0)),
-        ],
+        in_specs=[pl.BlockSpec(memory_space=pltpu.SMEM), whole, whole, whole, whole],
+        out_specs=[anywhere] * 3,
         out_shape=[
             jax.ShapeDtypeStruct((768, 768), F32),
             jax.ShapeDtypeStruct((192, 768), F32),
             jax.ShapeDtypeStruct((4, 3, 256, 1536), F32),
         ],
         scratch_shapes=[
+            vmem((192, 768), F32),
             vmem((2304, 768), BF16),
             vmem((1536, 768), BF16),
             vmem((1536, 1536), F8),
-            vmem((2, 384, 768), BF16),
-            vmem((2, 384, 1536), F8),
+            vmem((384, 768), BF16),
+            vmem((384, 768), BF16),
+            vmem((384, 1536), F8),
+            vmem((384, 1536), F8),
             vmem((2, 384, 2304), BF16),
             vmem((192, 2304), BF16),
             vmem((1024, 128), F32),
             vmem((512, 128), F32),
             vmem((8, 512), F32),
+            vmem((2, 2, 3, 128, 1536), F32),
             pltpu.SemaphoreType.DMA,
+            pltpu.SemaphoreType.DMA,
+            pltpu.SemaphoreType.DMA((2, 2)),
         ],
-        compiler_params=pltpu.CompilerParams(dimension_semantics=("arbitrary",), vmem_limit_bytes=40 << 20),
+        compiler_params=pltpu.CompilerParams(vmem_limit_bytes=40 << 20),
         cost_estimate=pl.CostEstimate(flops=3 * 10**10, bytes_accessed=3 * 10**7, transcendentals=0),
         name="panel_rows_and_trailing",
     )(slot_block, panel_pos, gathered, xcat, factor)
@@ -420,8 +449,8 @@
 
 
 def shards(panel_pos, trail_pos, slot_block):
-    factor, xcat, gathered = front_call(panel_pos, trail_pos)
-    return main_call(slot_block, panel_pos, gathered, xcat, factor, lambda: (lax.axis_index("prow"), lax.axis_index("pcol")))
+    factor, xcat, gathered, panel8 = front_call(panel_pos, trail_pos)
+    return main_call(slot_block, panel8, gathered, xcat, factor, lambda: (lax.axis_index("prow"), lax.axis_index("pcol")))
 
 
 def solution(mesh):

time: 66.8 us -> 65.5 us (0.981)
  Pallas kernels: 63.4 us -> 62.2 us
    pallas_call x1, Pallas kernels: 32.3 us -> 30.9 us  [main_call(): pl.pallas_call(functools.partial(kernel, ids=ids), in_specs=[pl.BlockSpec...]
where the time goes in v4:
time: 65.5 us; the launch traced here: 64.4 us
  Pallas kernels  62.2 us (95%)
  local copies, waits for them, and re-layouts  1.36 us (2%)
  between operations  0.82 us (1%)
    pallas_call x1, Pallas kernels, front_call(): pl.pallas_call(functools.partial(front_kernel, n_rows, n_cols), out_shape...  31.3 us
    pallas_call x1, Pallas kernels, main_call(): pl.pallas_call(functools.partial(kernel, ids=ids), in_specs=[pl.BlockSpec...  30.9 us
    unnamed x6, local copies, waits for them, and re-layouts  1.36 us

profile of v4, /device:TPU:0, one launch (start us, length us, event | category | flops | bytes accessed | tf_op | source)
XLA Modules:
  0.0 64.4 jit_solution(12057590961923037587)
XLA Ops:
  0.6 0.0 copy-start
  0.6 0.7 %copy-done = f32[3,256]{1,0:T(4,128)S(1)} copy-done((f32[3,256]{1,0:T(4,128)S(1)}, f32[3,256]{1,0:T(4,128)}, u32[]{:S(2)}) %copy-start) | copy-done | bytes 3096
  1.3 0.0 copy-start.1
  1.3 0.7 %copy-done.1 = f32[3,64]{1,0:T(4,128)S(1)} copy-done((f32[3,64]{1,0:T(4,128)S(1)}, f32[3,64]{1,0:T(4,128)}, u32[]{:S(2)}) %copy-start.1) | copy-done | bytes 792
  2.0 0.0 copy-start.2
  2.0 31.3 %factor_and_gather.1 = (f32[768,768]{1,0:T(8,128)S(1)}, bf16[768,2304]{1,0:T(8,128)(2,1)S(1)}, f32[16,8,3,64]{3,2,1,0:T(4,128)S(1)}, f32[8,256]{1,0:T(8,128)S(1)}) custom-call(f32[3,256]{1,0:T(4,128)S(1)} %copy-done, f32[3,64]{1,0:T(4,128)S(1)} %copy-done.1), custom_call_target="tpu_custom_call" | custom-call | flops 10000000000 | bytes 10000000 | tf_op jit(solution)/shard_map/factor_and_gather/pallas_call | solution.py:232
  33.3 0.0 copy-done.2
  33.3 30.9 %panel_rows_and_trailing.1 = (f32[768,768]{1,0:T(8,128)}, f32[192,768]{1,0:T(8,128)}, f32[4,3,256,1536]{3,2,1,0:T(8,128)}) custom-call(s32[32]{0:T(128)S(1)} %copy-done.2, f32[8,256]{1,0:T(8,128)S(1)} %get-tuple-element.10.panel_ref, f32[16,8,3,64]{3,2,1,0:T(4,128)S(1)} %get-tuple-element.11.g_ref, bf16[768,2304]{1,0:T(8,128)(2,1)S(1)} %get-tuple-element.12.xcat, ...), custom_call_target="tpu_custom_call" | custom-call | flops 30000001024 | bytes 30000000 | tf_op jit(solution)/shard_map/panel_rows_and_trailing/pallas_call | solution.py:416
Async XLA Ops:
  0.6 0.7 %copy-start = (f32[3,256]{1,0:T(4,128)S(1)}, f32[3,256]{1,0:T(4,128)}, u32[]{:S(2)}) copy-start(f32[3,256]{1,0:T(4,128)} %panel_ref.1) | copy-start | bytes 9220
  1.3 0.7 %copy-start.1 = (f32[3,64]{1,0:T(4,128)S(1)}, f32[3,64]{1,0:T(4,128)}, u32[]{:S(2)}) copy-start(f32[3,64]{1,0:T(4,128)} %own_ref.1) | copy-start | bytes 2308
  2.0 31.3 %copy-start.2 = (s32[32]{0:T(128)S(1)}, s32[32]{0:T(128)}, u32[]{:S(2)}) copy-start(s32[32]{0:T(128)} %slot_ref.1) | copy-start | bytes 388

commit v5 on v4

--- a/solution.py
+++ b/solution.py
@@ -168,7 +168,7 @@
 def lane_tile(g_ref, k, half):
     tiles = []
     for d in (4 * k + 2 * half, 4 * k + 2 * half + 1):
-        tiles.append(jnp.concatenate([g_ref[d % 16, d // 16], jnp.zeros((5, 64), F32)], axis=0))
+        tiles.append(jnp.concatenate([g_ref[d % 16, d // 16][:, :64], jnp.zeros((5, 64), F32)], axis=0))
     return jnp.concatenate(tiles, axis=1)
 
 
@@ -179,65 +179,79 @@
 MESH = pl.DeviceIdType.MESH
 
 
-def front_kernel(n_rows, n_cols, panel_ref, own_ref, l_ref, xcat, g_ref, p8, m_ref, d_ref, row_buf, lt_buf, l_buf, p3, pt, send_sem, recv_sem, local_sem, panel_sem):
+def front_kernel(x_ref, l_ref, xcat, g_ref, p8, m_ref, d_ref, row_buf, lt_buf, l_buf, pt, send_sem, recv_sem, local_sem):
     r = lax.axis_index("prow")
     c = lax.axis_index("pcol")
+    core, z, y, x = r % 2, r // 2, c % 4, c // 4
+    own_ref = x_ref.at[:, 256:384]
     local = pltpu.make_async_copy(own_ref, g_ref.at[c, r], local_sem)
     local.start()
-    panel_copy = pltpu.make_async_copy(panel_ref, p3, panel_sem)
-    panel_copy.start()
+    pair, line, plane = g_ref.at[c, pl.ds(2 * z, 2)], g_ref.at[c], g_ref.at[pl.ds(4 * x, 4)]
+    plan = [
+        [(own_ref, g_ref.at[c, r], (r + 1 - 2 * core, c))],
+        [(pair, pair, (lax.rem(z + i, 4) * 2 + core, c)) for i in range(1, 4)],
+        [(line, line, (r, x * 4 + lax.rem(y + i, 4))) for i in range(1, 4)],
+        [(plane, plane, (r, lax.rem(x + i, 4) * 4 + y)) for i in range(1, 4)],
+    ]
     barrier = pltpu.get_barrier_semaphore()
-    for i in range(1, n_rows):
-        pl.semaphore_signal(barrier, inc=1, device_id=(lax.rem(r + i, n_rows), c), device_id_type=MESH)
-    for i in range(1, n_cols):
-        pl.semaphore_signal(barrier, inc=1, device_id=(r, lax.rem(c + i, n_cols)), device_id_type=MESH)
-
-    def copy_to(src, dst, at, target):
-        return pltpu.make_async_remote_copy(
-            src_ref=src, dst_ref=dst, send_sem=send_sem.at[at], recv_sem=recv_sem.at[at], device_id=target, device_id_type=MESH
-        )
-
-    first = [copy_to(own_ref, g_ref.at[c, r], i, (lax.rem(r + i, n_rows), c)) for i in range(1, n_rows)]
-    second = [copy_to(g_ref.at[c], g_ref.at[c], n_rows + i, (r, lax.rem(c + i, n_cols))) for i in range(1, n_cols)]
+    for stage in plan:
+        for _, _, target in stage:
+            pl.semaphore_signal(barrier, inc=1, device_id=target, device_id_type=MESH)
+
+    stages = []
+    for k, stage in enumerate(plan):
+        stages.append([
+            pltpu.make_async_remote_copy(
+                src_ref=src,
+                dst_ref=dst,
+                send_sem=send_sem.at[3 * k + i],
+                recv_sem=recv_sem.at[3 * k + i],
+                device_id=target,
+                device_id_type=MESH,
+            )
+            for i, (src, dst, target) in enumerate(stage)
+        ])
 
     def after(p):
         @pl.when(p == 0)
         def _():
-            pl.semaphore_wait(barrier, n_rows + n_cols - 2)
-            for copy in first:
+            pl.semaphore_wait(barrier, 10)
+            for copy in stages[0]:
                 copy.start()
 
-        @pl.when(p == 1)
-        def _():
-            local.wait()
-            for copy in first:
-                copy.wait()
-            for copy in second:
-                copy.start()
+        for k in range(1, 4):
+
+            @pl.when(p == k)
+            def _():
+                if k == 1:
+                    local.wait()
+                for copy in stages[k - 1]:
+                    copy.wait()
+                for copy in stages[k]:
+                    copy.start()
 
     p8[...] = jnp.zeros((8, 256), F32)
-    panel_copy.wait()
-    p8[:3, :] = p3[...]
+    p8[:3, :] = x_ref[:, :256]
     for half in range(2):
         pt[128 * half : 128 * half + 128, :] = transposed(p8[:, 128 * half : 128 * half + 128])
     chol(p8, pt, m_ref, d_ref, row_buf, lt_buf, l_buf, xcat, after)
     store_factor(l_ref, l_buf)
-    for copy in second:
+    for copy in stages[3]:
         copy.wait()
 
 
 def front_call(panel_pos, own):
-    n_rows, n_cols = lax.axis_size("prow"), lax.axis_size("pcol")
     vmem = pl.BlockSpec(memory_space=pltpu.VMEM)
+    together = jnp.concatenate([panel_pos, jnp.pad(own, ((0, 0), (0, 128 - own.shape[1])))], axis=1)
     return pl.pallas_call(
-        functools.partial(front_kernel, n_rows, n_cols),
+        front_kernel,
         out_shape=[
             jax.ShapeDtypeStruct((768, 768), F32),
             jax.ShapeDtypeStruct((768, 2304), BF16),
-            jax.ShapeDtypeStruct((n_cols, n_rows) + own.shape, F32),
+            jax.ShapeDtypeStruct((16, 8, 3, 128), F32),
             jax.ShapeDtypeStruct((8, 256), F32),
         ],
-        in_specs=[pl.BlockSpec(memory_space=pltpu.HBM)] * 2,
+        in_specs=[vmem],
         out_specs=[vmem] * 4,
         cost_estimate=pl.CostEstimate(flops=10**10, bytes_accessed=10**7, transcendentals=0),
         scratch_shapes=[
@@ -246,16 +260,14 @@
             pltpu.VMEM((128, 768), F32),
             pltpu.VMEM((640, 128), F32),
             pltpu.VMEM((1408, 768), F32),
-            pltpu.VMEM((3, 256), F32),
             pltpu.VMEM((256, 128), F32),
-            pltpu.SemaphoreType.DMA((n_rows + n_cols,)),
-            pltpu.SemaphoreType.DMA((n_rows + n_cols,)),
-            pltpu.SemaphoreType.DMA,
+            pltpu.SemaphoreType.DMA((12,)),
+            pltpu.SemaphoreType.DMA((12,)),
             pltpu.SemaphoreType.DMA,
         ],
         compiler_params=pltpu.CompilerParams(collective_id=0, has_side_effects=True, vmem_limit_bytes=40 << 20),
         name="factor_and_gather",
-    )(panel_pos, own)
+    )(together)
 
 
 def panel_entries(rows, panel_ref, bcat):

time: 65.5 us -> 63.6 us (0.971); the launches traced: 64.4 us -> 63.5 us
  local copies, waits for them, and re-layouts: 1.36 us -> 0.01 us
  other arithmetic: 0 us -> 0.71 us
    unnamed x6 -> x2, local copies, waits for them, and re-layouts: 1.36 us -> 0.01 us
    concatenate x0 -> x1, other arithmetic: none -> 0.71 us  [front_call(): jnp.concatenate([panel_pos, jnp.pad(own, ((0, 0), (0, 128 - own.shape[1])...]
where the time goes in v5:
time: 63.6 us; the launch traced here: 63.5 us
  Pallas kernels  62 us (97%)
  between operations  0.81 us (1%)
  other arithmetic  0.71 us (1%)
    pallas_call x1, Pallas kernels, front_call(): pl.pallas_call(front_kernel, out_shape=[jax.ShapeDtypeStruct((768, 768),...  31.2 us
    pallas_call x1, Pallas kernels, main_call(): pl.pallas_call(functools.partial(kernel, ids=ids), in_specs=[pl.BlockSpec...  30.7 us

profile of v5, /device:TPU:0, one launch (start us, length us, event | category | flops | bytes accessed | tf_op | source)
XLA Modules:
  0.0 63.5 jit_solution(2014596530213775814)
XLA Ops:
  0.6 0.7 %select_maximum_fusion.x_ref = f32[3,384]{1,0:T(4,128)S(1)} fusion(f32[3,64]{1,0:T(4,128)} %param.4, f32[3,256]{1,0:T(4,128)} %param.3), kind=kLoop, calls=%fused_computation | loop fusion | flops 3456 | bytes 8448 | tf_op jit(solution)/shard_map/concatenate | solution.py:245
  1.3 0.0 copy-start
  1.3 31.2 %factor_and_gather.1 = (f32[768,768]{1,0:T(8,128)S(1)}, bf16[768,2304]{1,0:T(8,128)(2,1)S(1)}, f32[16,8,3,128]{3,2,1,0:T(4,128)S(1)}, f32[8,256]{1,0:T(8,128)S(1)}) custom-call(f32[3,384]{1,0:T(4,128)S(1)} %select_maximum_fusion.x_ref), custom_call_target="tpu_custom_call" | custom-call | flops 10000000000 | bytes 10000000 | tf_op jit(solution)/shard_map/factor_and_gather/pallas_call | solution.py:246
  32.6 0.0 copy-done
  32.6 30.7 %panel_rows_and_trailing.1 = (f32[768,768]{1,0:T(8,128)}, f32[192,768]{1,0:T(8,128)}, f32[4,3,256,1536]{3,2,1,0:T(8,128)}) custom-call(s32[32]{0:T(128)S(1)} %copy-done, f32[8,256]{1,0:T(8,128)S(1)} %get-tuple-element.10.panel_ref, f32[16,8,3,128]{3,2,1,0:T(4,128)S(1)} %get-tuple-element.11.g_ref, bf16[768,2304]{1,0:T(8,128)(2,1)S(1)} %get-tuple-element.12.xcat, ...), custom_call_target="tpu_custom_call" | custom-call | flops 30000001024 | bytes 30000000 | tf_op jit(solution)/shard_map/panel_rows_and_trailing/pallas_call | solution.py:428
Async XLA Ops:
  1.3 31.2 %copy-start = (s32[32]{0:T(128)S(1)}, s32[32]{0:T(128)}, u32[]{:S(2)}) copy-start(s32[32]{0:T(128)} %slot_ref.1) | copy-start | bytes 388

commit v6 on v5

--- a/solution.py
+++ b/solution.py
@@ -335,16 +335,17 @@
 
     def inverse_of_diag():
         for b in range(3):
-            for a in range(3):
-                k = slice(256 * max(a, b), 768)
+            for a in range(b + 1):
+                k = slice(256 * b, 768)
                 hi = lambda q: xcat[k, 768 * q : 768 * q + 256]
                 lo = lambda q: xcat[k, 768 * q + 512 : 768 * q + 768]
                 w = pre_split_dot((hi(a), lo(a)), (hi(b), lo(b)), TN)
-                wh, wl = split(w)
-                at = slice(256 * b, 256 * b + 256)
-                wcat[768 * a : 768 * a + 256, at] = wh
-                wcat[768 * a + 256 : 768 * a + 512, at] = wh
-                wcat[768 * a + 512 : 768 * a + 768, at] = wl
+                for row, col, block in [(a, b, w)] + ([(b, a, w.T)] if a < b else []):
+                    wh, wl = split(block)
+                    at = slice(256 * col, 256 * col + 256)
+                    wcat[768 * row : 768 * row + 256, at] = wh
+                    wcat[768 * row + 256 : 768 * row + 512, at] = wh
+                    wcat[768 * row + 512 : 768 * row + 768, at] = wl
 
     def own_rows():
         for h in range(3):

time: 63.6 us -> 63.4 us (level)
  no operation moved by 1% of the time
where the time goes in v6:
time: 63.4 us; the launch traced here: 63.3 us
  Pallas kernels  61.8 us (97%)
  between operations  0.81 us (1%)
  other arithmetic  0.71 us (1%)
    pallas_call x1, Pallas kernels, front_call(): pl.pallas_call(front_kernel, out_shape=[jax.ShapeDtypeStruct((768, 768),...  31.2 us
    pallas_call x1, Pallas kernels, main_call(): pl.pallas_call(functools.partial(kernel, ids=ids), in_specs=[pl.BlockSpec...  30.5 us

profile of v6, /device:TPU:0, one launch (start us, length us, event | category | flops | bytes accessed | tf_op | source)
XLA Modules:
  0.0 63.3 jit_solution(1525578633770912676)
XLA Ops:
  0.6 0.7 %select_maximum_fusion.x_ref = f32[3,384]{1,0:T(4,128)S(1)} fusion(f32[3,64]{1,0:T(4,128)} %param.4, f32[3,256]{1,0:T(4,128)} %param.3), kind=kLoop, calls=%fused_computation | loop fusion | flops 3456 | bytes 8448 | tf_op jit(solution)/shard_map/concatenate | solution.py:245
  1.3 0.0 copy-start
  1.3 31.2 %factor_and_gather.1 = (f32[768,768]{1,0:T(8,128)S(1)}, bf16[768,2304]{1,0:T(8,128)(2,1)S(1)}, f32[16,8,3,128]{3,2,1,0:T(4,128)S(1)}, f32[8,256]{1,0:T(8,128)S(1)}) custom-call(f32[3,384]{1,0:T(4,128)S(1)} %select_maximum_fusion.x_ref), custom_call_target="tpu_custom_call" | custom-call | flops 10000000000 | bytes 10000000 | tf_op jit(solution)/shard_map/factor_and_gather/pallas_call | solution.py:246
  32.6 0.0 copy-done
  32.6 30.5 %panel_rows_and_trailing.1 = (f32[768,768]{1,0:T(8,128)}, f32[192,768]{1,0:T(8,128)}, f32[4,3,256,1536]{3,2,1,0:T(8,128)}) custom-call(s32[32]{0:T(128)S(1)} %copy-done, f32[8,256]{1,0:T(8,128)S(1)} %get-tuple-element.10.panel_ref, f32[16,8,3,128]{3,2,1,0:T(4,128)S(1)} %get-tuple-element.11.g_ref, bf16[768,2304]{1,0:T(8,128)(2,1)S(1)} %get-tuple-element.12.xcat, ...), custom_call_target="tpu_custom_call" | custom-call | flops 30000001024 | bytes 30000000 | tf_op jit(solution)/shard_map/panel_rows_and_trailing/pallas_call | solution.py:429
Async XLA Ops:
  1.3 31.2 %copy-start = (s32[32]{0:T(128)S(1)}, s32[32]{0:T(128)}, u32[]{:S(2)}) copy-start(s32[32]{0:T(128)} %slot_ref.1) | copy-start | bytes 388
